TPU v7x, 256 devices: a whole 4x4x8 slice. The times are simulated.
256 devices in a mesh: dom: 128 (over x, y_lo, z, core), feat: 2 (over y_hi).
Axes of the slice: x: 4, y: 4 (y_hi: 2, y_lo: 2; y = y_hi * 2 + y_lo), z: 8, core: 2. Of those that a mesh axis runs over, the one named last changes fastest.
Arguments:
- features: float32 [262144, 512], P('dom', 'feat'), may hold values from -6 to 6
- infill_mask: int32 [262144], P('dom'), may hold values 0 or 1
- mask_token: float32 [512], P('feat'), may hold values from -4 to 4
- local_rows: int32 [128, 64], P('dom'), may hold values from 0 to 15
- local_cols: int32 [128, 64], P('dom'), may hold values from 12 to 35, as said below
- local_tiles: float32 [128, 64, 128, 128], P('dom'), may hold values from -0.1875 to 0.1875
- hub_ids: int32 [4096], P('dom'), may hold values from 0 to 262143, as said below
- hub_count: int32 [128], P('dom'), may hold values from 16 to 64, as said below
- hub_rows: int32 [128, 64], P('dom'), may hold values from 0 to 15
- hub_panels: int32 [128, 64], P('dom'), may hold values from 0 to 31
- hub_tiles: float32 [128, 64, 128, 128], P('dom'), may hold values from -0.1875 to 0.1875
- mix_weight: float32 [512, 512], P(None, 'feat'), may hold values from -0.25 to 0.25
- mix_bias: float32 [512], P('feat'), may hold values from -3 to 3
- norm_gain: float32 [512], P('feat'), may hold values from 0.25 to 1.75
Outputs:
- updated: float32 [262144, 512], P('dom', 'feat')
Inputs may be any that keep to these rules, and one draw needn't show every extreme that they name: `hub_ids`: index block k of 32 entries holds distinct vertices of partition k. `hub_count`: some partition has all 64 slots live. `local_cols`: each local tile's column block differs from its row block plus 2048 // 128 by at most 4, and in every partition by exactly 4 on both sides.
All inputs are finite; a program needn't handle non-finite values. No bound on the sum of `infill_mask` on one device may be relied on, other than what follows from the above.
Results may differ from a plain program's by a relative error of at most 0.0003.
Values sent between devices are 32-bit elements; how exact they have to be, the bound alone decides.
No kernel may reach another device: no remote copies, remote signals or barrier semaphores. Data moves between devices by JAX's collectives and lax.ppermute only.
A program may use at most 128 MiB of HBM per device.

v0:
```python
import jax
import jax.numpy as jnp
from jax import lax
from jax.sharding import PartitionSpec as P


def with_halo(cells, sides, width):
    for axis, dim in sides:
        count = lax.axis_size(axis)
        ends = count - 1
        head = lax.slice_in_dim(cells, 0, width, axis=dim)
        tail = lax.slice_in_dim(cells, cells.shape[dim] - width, cells.shape[dim], axis=dim)
        cells = jnp.concatenate(
            [
                lax.ppermute(tail, axis, [(i, (i + 1) % count) for i in range(ends)]),
                cells,
                lax.ppermute(head, axis, [((i + 1) % count, i) for i in range(ends)]),
            ],
            axis=dim,
        )
    return cells


def block_sum(row_ids, tiles, picked, blocks, weights):
    highest = lax.Precision.HIGHEST
    products = jnp.einsum("tij,tjf->tif", tiles, picked, precision=highest)
    onehot = (row_ids[None, :] == jnp.arange(blocks, dtype=jnp.int32)[:, None]).astype(
        jnp.float32
    ) * weights[None, :]
    return jnp.einsum("rt,tif->rif", onehot, products, precision=highest)


def shards(
    features,
    infill_mask,
    mask_token,
    local_rows,
    local_cols,
    local_tiles,
    hub_ids,
    hub_count,
    hub_rows,
    hub_panels,
    hub_tiles,
    mix_weight,
    mix_bias,
    norm_gain,
):
    highest = lax.Precision.HIGHEST
    rows = features.shape[0]
    half = features.shape[1]
    blocks = rows // 128
    first_row = lax.axis_index("dom") * rows
    filled = jnp.where(infill_mask[:, None] == 1, mask_token[None, :], features)
    extended = with_halo(filled, (("dom", 0),), rows)
    ext_blocks = extended.reshape(3 * blocks, 128, half)
    col_ids = local_cols[0]
    owned_hubs = filled[hub_ids - first_row]
    every_hub = lax.all_gather(owned_hubs, "dom", axis=0, tiled=True)
    panels = every_hub.reshape(-1, 128, half)
    loc_count = local_rows.shape[1]
    slot_count = hub_rows.shape[1]
    total = block_sum(
        local_rows[0],
        local_tiles[0],
        ext_blocks[col_ids],
        blocks,
        jnp.ones((loc_count,), jnp.float32),
    )
    live = (jnp.arange(slot_count, dtype=jnp.int32) < hub_count[0]).astype(jnp.float32)
    total = total + block_sum(hub_rows[0], hub_tiles[0], panels[hub_panels[0]], blocks, live)
    aggregate = total.reshape(rows, half)
    full_aggregate = lax.all_gather(aggregate, "feat", axis=1, tiled=True)
    pre = jnp.dot(full_aggregate, mix_weight, precision=highest) + mix_bias[None, :]
    hidden = filled + jax.nn.silu(pre)
    sum_one, sum_two = lax.psum((jnp.sum(hidden, 1), jnp.sum(hidden * hidden, 1)), "feat")
    width = half * lax.axis_size("feat")
    mean_val = (sum_one / width)[:, None]
    square_val = (sum_two / width)[:, None]
    scale_val = lax.rsqrt(square_val - mean_val * mean_val + 1e-05)
    return (hidden - mean_val) * scale_val * norm_gain[None, :]


def solution(mesh):
    in_specs = (
        P("dom", "feat"),
        P("dom"),
        P("feat"),
        P("dom", None),
        P("dom", None),
        P("dom", None, None, None),
        P("dom"),
        P("dom"),
        P("dom", None),
        P("dom", None),
        P("dom", None, None, None),
        P(None, "feat"),
        P("feat"),
        P("feat"),
    )
    out_specs = P("dom", "feat")
    return jax.shard_map(shards, mesh=mesh, in_specs=in_specs, out_specs=out_specs, check_vma=False)
```

profile of v0, /device:TPU:8, one launch (start us, length us, event | category | flops | bytes accessed | tf_op | source)
XLA Modules:
  0.0 389.8 jit_solution(8485153833371458331)
XLA Ops:
  6.6 2.9 copy.18
  11.4 1.8 copy.20
  13.2 2.8 gather_fusion.1
  16.1 7.1 %collective-permute-start.1 = (f32[2048,256]{0,1:T(8,128)S(1)}, f32[2048,256]{0,1:T(8,128)S(1)}, u32[]{:S(2)}, u32[]{:S(2)}) collective-permute-start(f32[2048,256]{0,1:T(8,128)S(1)} %broadcast_select_fusion), channel_id=1, source_target_pairs={{2,0},{4,2},{6,4},{8,6},{10,8},{12,10},{14,12},{16,14},{18,16},{20... | collective-permute-start | bytes 6291464 | tf_op jit(solution)/shard_map/ppermute | solution.py:17
  23.2 1.9 collective-permute-start
  25.8 20.9 %collective-permute-done.1 = f32[2048,256]{0,1:T(8,128)S(1)} collective-permute-done((f32[2048,256]{0,1:T(8,128)S(1)}, f32[2048,256]{0,1:T(8,128)S(1)}, u32[]{:S(2)}, u32[]{:S(2)}) %collective-permute-start.1) | collective-permute-done | bytes 2097184 | tf_op jit(solution)/shard_map/ppermute | solution.py:17
  46.7 5.9 %collective-permute-done = f32[2048,256]{0,1:T(8,128)S(1)} collective-permute-done((f32[2048,256]{0,1:T(8,128)S(1)}, f32[2048,256]{0,1:T(8,128)S(1)}, u32[]{:S(2)}, u32[]{:S(2)}) %collective-permute-start) | collective-permute-done | bytes 2097184 | tf_op jit(solution)/shard_map/ppermute | solution.py:15
  52.6 3.1 pad_maximum_fusion
  55.7 6.6 %copy.25 = f32[6144,256]{1,0:T(8,128)} copy(f32[6144,256]{0,1:T(8,128)} %pad_maximum_fusion) | data formatting | bytes 12582912 | tf_op jit(solution)/shard_map/reshape | solution.py:56
  62.3 7.1 %gather_fusion = f32[64,128,256]{2,1,0:T(8,128)} fusion(f32[48,128,256]{2,1,0:T(8,128)} %bitcast.39, s32[1024]{0:T(1024)S(1)} %pad_clamp_fusion.2), kind=kCustom, calls=%fused_computation | custom fusion | bytes 16777472 | tf_op jit(solution)/shard_map/gather | solution.py:66
  69.4 19.6 %fusion.6 = f32[64,256,128]{2,1,0:T(8,128)} fusion(f32[64,128,256]{2,1,0:T(8,128)} %gather_fusion, f32[1,64,128,128]{3,2,1,0:T(8,128)} %param.19), kind=kOutput, calls=%fused_computation.10 | convolution fusion | flops 3221225472 | bytes 20971520 | tf_op jit(solution)/shard_map/tij,tjf->tif/dot_general | solution.py:26
  89.0 9.2 %copy.23 = f32[64,256,128]{1,0,2:T(8,128)} copy(f32[64,256,128]{2,1,0:T(8,128)} %fusion.6) | data formatting | bytes 16777216 | tf_op jit(solution)/shard_map/tij,tjf->tif/dot_general | solution.py:26
  98.2 151.7 %all-gather.6.cloned.1.call-done = f32[4096,256]{1,0:T(8,128)} async-done(((f32[32,256]{1,0:T(8,128)}), f32[4096,256]{1,0:T(8,128)}) %all-gather.6.cloned.1.call-update) | async-done | bytes 4194320 | tf_op jit(solution)/shard_map/all_gather | solution.py:59
  250.0 6.5 %gather_fusion.2 = f32[64,128,256]{2,1,0:T(8,128)} fusion(f32[32,128,256]{2,1,0:T(8,128)} %bitcast.40, s32[1024]{0:T(1024)S(1)} %pad_clamp_fusion), kind=kCustom, calls=%fused_computation.2 | custom fusion | bytes 16777472 | tf_op jit(solution)/shard_map/gather | solution.py:71
  256.5 19.6 %fusion.4 = f32[64,256,128]{2,1,0:T(8,128)} fusion(f32[64,128,256]{2,1,0:T(8,128)} %gather_fusion.2, f32[1,64,128,128]{3,2,1,0:T(8,128)} %param.24), kind=kOutput, calls=%fused_computation.8 | convolution fusion | flops 3221225472 | bytes 20971520 | tf_op jit(solution)/shard_map/tij,tjf->tif/dot_general | solution.py:26
  276.1 9.3 %copy.24 = f32[64,256,128]{1,0,2:T(8,128)} copy(f32[64,256,128]{2,1,0:T(8,128)} %fusion.4) | data formatting | bytes 16777216 | tf_op jit(solution)/shard_map/tij,tjf->tif/dot_general | solution.py:26
  285.3 6.4 %fusion = f32[16,128,256]{2,0,1:T(8,128)S(1)} fusion(f32[64,256,128]{1,0,2:T(8,128)} %copy.24, f32[64]{0:T(128)S(1)} %compare_convert_fusion, s32[64]{0:T(128)S(1)} %bitcast.42), kind=kOutput, calls=%fused_computation.3 | convolution fusion | flops 402655232 | bytes 10486272 | tf_op jit(solution)/shard_map/rt,tif->rif/dot_general | solution.py:30
  291.8 5.4 %fusion.8 = f32[16,128,256]{2,0,1:T(8,128)S(1)} fusion(f32[16,128,256]{2,0,1:T(8,128)S(1)} %fusion, f32[64,256,128]{1,0,2:T(8,128)} %copy.23, s32[64]{0:T(128)S(1)} %bitcast.43), kind=kOutput, calls=%fused_computation.16 | convolution fusion | flops 403178496 | bytes 12583168 | tf_op jit(solution)/shard_map/rt,tif->rif/dot_general | solution.py:30
  297.2 2.5 copy.21
  299.8 62.0 %all-gather.4.cloned.1.call-done = f32[2048,512]{1,0:T(8,128)} async-done(((f32[2048,256]{1,0:T(8,128)}), f32[2048,512]{1,0:T(8,128)}) %all-gather.4.cloned.1.call-update) | async-done | bytes 4194320 | tf_op jit(solution)/shard_map/all_gather | solution.py:73
  361.8 7.9 %fusion.22 = (f32[2048]{0:T(1024)S(1)}, f32[2048]{0:T(1024)S(1)}, f32[2048,256]{0,1:T(8,128)}) fusion(f32[2048,256]{0,1:T(8,128)S(1)} %broadcast_select_fusion, f32[256]{0:T(256)S(1)} %copy-done.6, f32[2048,512]{1,0:T(8,128)} %all-gather.4.cloned.1.call-done, f32[512,256]{1,0:T(8,128)S(1)} %copy-done), kind=kOutput, calls=%fused_computation.40 | convolution fusion | flops 3225939968 | bytes 8930304 | tf_op jit(solution)/shard_map/dot_general | solution.py:74
  369.7 9.5 %all-reduce = (f32[2048]{0:T(1024)S(1)}, f32[2048]{0:T(1024)S(1)}) all-reduce(f32[2048]{0:T(1024)S(1)} %get-tuple-element.6, f32[2048]{0:T(1024)S(1)} %get-tuple-element.5), channel_id=1, replica_groups=mesh['dom'=128,'feat'=2] {'feat'}, use_global_device_ids=true, to_apply=%region_3.4 | all-reduce | flops 4096 | bytes 32768 | tf_op jit(solution)/shard_map/psum | solution.py:76
  379.2 1.9 multiply_multiply_fusion
  381.1 1.8 copy.22
  (34 shorter events, 2.0 us)
Async XLA Ops:
  6.5 355.3 %copy-start = (f32[512,256]{1,0:T(8,128)S(1)}, f32[512,256]{1,0:T(8,128)}, u32[]{:S(2)}) copy-start(f32[512,256]{1,0:T(8,128)} %param.25) | copy-start | bytes 1572868
  6.5 3.0 copy-start.1
  6.5 3.0 copy-start.2
  6.5 243.4 %all-gather.6.cloned.1.call-start = ((), (), s32[]{:S(2)}) async-start(), calls=%async_computation.1 | async-start | bytes 4227072 | tf_op jit(solution)/shard_map/all_gather | solution.py:59
  9.5 3.7 copy-start.7
  9.5 16.2 %copy-start.8 = (s32[1,64]{1,0:T(1,128)S(1)}, s32[1,64]{1,0:T(1,128)}, u32[]{:S(2)}) copy-start(s32[1,64]{1,0:T(1,128)} %param.23) | copy-start | bytes 772
  9.5 16.3 %copy-start.9 = (s32[1,64]{1,0:T(1,128)S(1)}, s32[1,64]{1,0:T(1,128)}, u32[]{:S(2)}) copy-start(s32[1,64]{1,0:T(1,128)} %param.18) | copy-start | bytes 772
  16.0 345.8 %all-gather.4.cloned.1.call-start = ((), (), s32[]{:S(2)}) async-start(), calls=%async_computation | async-start | bytes 6291456 | tf_op jit(solution)/shard_map/all_gather | solution.py:73
  16.1 30.6 %collective-permute-start.1 = (f32[2048,256]{0,1:T(8,128)S(1)}, f32[2048,256]{0,1:T(8,128)S(1)}, u32[]{:S(2)}, u32[]{:S(2)}) collective-permute-start(f32[2048,256]{0,1:T(8,128)S(1)} %broadcast_select_fusion), channel_id=1, source_target_pairs={{2,0},{4,2},{6,4},{8,6},{10,8},{12,10},{14,12},{16,14},{18,16},{20... | collective-permute-start | bytes 6291464 | tf_op jit(solution)/shard_map/ppermute | solution.py:17
  23.2 29.5 %collective-permute-start = (f32[2048,256]{0,1:T(8,128)S(1)}, f32[2048,256]{0,1:T(8,128)S(1)}, u32[]{:S(2)}, u32[]{:S(2)}) collective-permute-start(f32[2048,256]{0,1:T(8,128)S(1)} %broadcast_select_fusion), channel_id=1, source_target_pairs={{0,2},{2,4},{4,6},{6,8},{8,10},{10,12},{12,14},{14,16},{16,18},{18... | collective-permute-start | bytes 6291464 | tf_op jit(solution)/shard_map/ppermute | solution.py:15
  276.1 9.3 %copy-start.4 = (s32[1,64]{1,0:T(1,128)S(1)}, s32[1,64]{1,0:T(1,128)}, u32[]{:S(2)}) copy-start(s32[1,64]{1,0:T(1,128)} %param.22) | copy-start | bytes 772
  285.3 6.4 %copy-start.5 = (s32[1,64]{1,0:T(1,128)S(1)}, s32[1,64]{1,0:T(1,128)}, u32[]{:S(2)}) copy-start(s32[1,64]{1,0:T(1,128)} %param.17) | copy-start | bytes 772
  297.2 64.6 %copy-start.6 = (f32[256]{0:T(256)S(1)}, f32[256]{0:T(256)}, u32[]{:S(2)}) copy-start(f32[256]{0:T(256)} %param.26) | copy-start | bytes 3076
  299.8 79.4 %copy-start.3 = (f32[256]{0:T(256)S(1)}, f32[256]{0:T(256)}, u32[]{:S(2)}) copy-start(f32[256]{0:T(256)} %param.27) | copy-start | bytes 3076
Sparse Core Ops, SparseCore 0:
  16.1 233.7 all-gather.5
  299.9 61.8 all-gather.3
where the time goes:
time: 391 us; the launch traced here: 390 us
  waiting for transfers between devices  241 us (62%)
  matrix products  58.9 us (15%)
  local copies, waits for them, and re-layouts  50.7 us (13%)
  between operations  14.2 us (4%)
  blocking collectives  9.5 us (2%)
  starting transfers between devices  9.05 us (2%)
  other arithmetic  6.81 us (2%)
    all_gather x1, waiting for transfers between devices, shards(): every_hub = lax.all_gather(owned_hubs, 'dom', axis=0, tiled=True)  152 us
    all_gather x1, waiting for transfers between devices, shards(): full_aggregate = lax.all_gather(aggregate, 'feat', axis=1, tiled=True)  62 us
    dot_general x2, matrix products, block_sum(): products = jnp.einsum('tij,tjf->tif', tiles, picked, precision=highest)  39.2 us
    ppermute x1, waiting for transfers between devices, with_halo(): lax.ppermute(head, axis, [((i + 1) % count, i) for i in range(ends)])  20.9 us
    dot_general x2, local copies, waits for them, and re-layouts, block_sum(): products = jnp.einsum('tij,tjf->tif', tiles, picked, precision=highest)  18.5 us
    dot_general x2, matrix products, block_sum(): return jnp.einsum('rt,tif->rif', onehot, products, precision=highest)  11.9 us
    psum x1, blocking collectives, shards(): lax.psum((jnp.sum(hidden, 1), jnp.sum(hidden * hidden, 1)), 'feat')  9.5 us
    dot_general x1, matrix products, shards(): jnp.dot(full_aggregate, mix_weight, precision=highest) + mix_bias[None, :]  7.9 us
  transfers between devices with their start and end apart: 4, of which 4 were waited for; matrix products, arithmetic and copies ran while one was open for 12% of the time, Pallas kernels for 0%

commit v1 on v0

v1 whole, which is shorter than its diff:
```python
import jax
import jax.numpy as jnp
from jax import lax
from jax.experimental import pallas as pl
from jax.experimental.pallas import tpu as pltpu
from jax.sharding import PartitionSpec as P

NX, NYL, NZ, NC = 4, 2, 8, 2
BOTH = ("dom", "feat")
F32 = jnp.float32
BF = jnp.bfloat16
SMEM = pl.BlockSpec(memory_space=pltpu.SMEM)
VMEM = pl.BlockSpec(memory_space=pltpu.VMEM)
ANY = pl.BlockSpec(memory_space=pl.ANY)


def dom_index(x, yl, z, c):
    return ((x * NYL + yl) * NZ + z) * NC + c


def shift(move):
    pairs = []
    for x in range(NX):
        for yl in range(NYL):
            for z in range(NZ):
                for c in range(NC):
                    for f in range(2):
                        tx, tyl, tz, tc, tf = move(x, yl, z, c, f)
                        pairs.append(
                            (
                                dom_index(x, yl, z, c) * 2 + f,
                                dom_index(tx % NX, tyl, tz % NZ, tc) * 2 + tf,
                            )
                        )
    return pairs


def send(value, move):
    return lax.ppermute(value, BOTH, shift(move))


def place():
    dom = lax.axis_index("dom")
    c = dom % NC
    z = (dom // NC) % NZ
    yl = (dom // (NC * NZ)) % NYL
    x = dom // (NC * NZ * NYL)
    return x, yl, z, c


def split(a):
    hi = a.astype(BF)
    return hi, (a - hi.astype(F32)).astype(BF)


def dot(a, b):
    return jnp.dot(a, b, preferred_element_type=F32)


def hub_rows_kernel(ids, mask, features, token, out, sems):
    first = lax.axis_index("dom") * features.shape[0]
    count = out.shape[0]
    copies = []
    for i in range(count):
        row = ids[i] - first
        copies.append(
            pltpu.make_async_copy(features.at[pl.ds(row, 1)], out.at[pl.ds(i, 1)], sems.at[i])
        )
        copies[-1].start()
    for i in range(count):
        copies[i].wait()
    for i in range(count):
        row = ids[i] - first

        @pl.when(mask[row] == 1)
        def _():
            out[pl.ds(i, 1), :] = token[...]


def hub_rows_of(hub_ids, infill_mask, features, mask_token):
    count = hub_ids.shape[0]
    return pl.pallas_call(
        hub_rows_kernel,
        out_shape=jax.ShapeDtypeStruct((count, features.shape[1]), F32),
        in_specs=[SMEM, SMEM, ANY, VMEM],
        out_specs=VMEM,
        scratch_shapes=[pltpu.SemaphoreType.DMA((count,))],
        name="hub_rows",
    )(hub_ids, infill_mask, features, mask_token[None, :])


def mix_rows(xf, xg, weight):
    f = lax.axis_index("feat")
    half = xf.shape[1]
    wf = weight[pl.ds(pl.multiple_of(f * half, half), half), :]
    wg = weight[pl.ds(pl.multiple_of((1 - f) * half, half), half), :]
    wfh, wfl = split(wf)
    wgh, wgl = split(wg)
    right = jnp.concatenate([wfh, wfl, wfh, wgh, wgl, wgh], 0)
    fh, fl = split(xf)
    gh, gl = split(xg)
    left = jnp.concatenate([fh, fh, fl, gh, gh, gl], 1)
    return dot(left, right)


def mix_kernel(xf, xg, weight, out):
    step = 256
    for i in range(xf.shape[0] // step):
        at = pl.ds(i * step, step)
        out[at, :] = mix_rows(xf[at, :], xg[at, :], weight)


def mix(xf, xg, weight):
    rows, half = xf.shape
    return pl.pallas_call(
        mix_kernel,
        out_shape=jax.ShapeDtypeStruct((rows, half), F32),
        in_specs=[VMEM] * 3,
        out_specs=VMEM,
        name="mix_rows",
        cost_estimate=pl.CostEstimate(
            flops=rows * half * half * 12, bytes_accessed=rows * half * 12, transcendentals=0
        ),
        compiler_params=pltpu.CompilerParams(vmem_limit_bytes=16 << 20),
    )(xf, xg, weight)


def mix_hub_kernel(own_f, own_g, other_f, other_g, weight, out):
    count = own_f.shape[0]
    yl = place()[1]
    xf = jnp.concatenate([own_f[...], other_f[...]], 0)
    xg = jnp.concatenate([own_g[...], other_g[...]], 0)
    y = mix_rows(xf, xg, weight)
    out[pl.ds(pl.multiple_of(yl * count, count), count), :] = y[:count]
    out[pl.ds(pl.multiple_of((1 - yl) * count, count), count), :] = y[count:]


def mix_hub(own_f, own_g, other_f, other_g, weight):
    count, half = own_f.shape
    return pl.pallas_call(
        mix_hub_kernel,
        out_shape=jax.ShapeDtypeStruct((2 * count, half), F32),
        in_specs=[VMEM] * 5,
        out_specs=VMEM,
        name="mix_hub",
    )(own_f, own_g, other_f, other_g, weight)


def tile_product(tile, y):
    ah, al = split(tile)
    yh, yl = split(y)
    return dot(jnp.concatenate([ah, ah, al], 1), jnp.concatenate([yh, yl, yh], 0))


UNROLL = 8


def local_kernel(rows, cols, tiles, prev, first, mid, last, after, total, ext):
    total[...] = jnp.zeros_like(total)
    at = 0
    for part in (prev, first, mid, last, after):
        n = part.shape[0] // 128
        ext[pl.ds(at, n)] = part[...].reshape(n, 128, part.shape[1])
        at += n
    low = total.shape[0] - (ext.shape[0] - total.shape[0]) // 2

    def step(i, carry):
        products = []
        for u in range(UNROLL):
            t = i * UNROLL + u
            products.append(tile_product(tiles[t], ext[cols[0, t] - low]))
        for u in range(UNROLL):
            total[rows[0, i * UNROLL + u]] += products[u]
        return carry

    lax.fori_loop(0, tiles.shape[0] // UNROLL, step, 0)


def local_sum(rows, cols, tiles, parts, blocks):
    half = parts[0].shape[1]
    depth = sum(p.shape[0] for p in parts) // 128
    count = tiles.shape[0]
    return pl.pallas_call(
        local_kernel,
        out_shape=jax.ShapeDtypeStruct((blocks, 128, half), F32),
        in_specs=[SMEM, SMEM] + [VMEM] * 6,
        out_specs=VMEM,
        scratch_shapes=[pltpu.VMEM((depth, 128, half), F32)],
        name="local_tiles",
        cost_estimate=pl.CostEstimate(
            flops=count * 128 * 128 * half * 6, bytes_accessed=12 << 20, transcendentals=0
        ),
        compiler_params=pltpu.CompilerParams(vmem_limit_bytes=24 << 20),
    )(rows, cols, tiles, *parts)


def hub_kernel(
    count_ref, rows, panels, tiles, total_in, filled, bias, *rest
):
    parts = rest[: 2 * NX]
    hidden, stats, total, held, sems = rest[2 * NX :]
    copies = []
    for side in range(2):
        for dx in range(NX):
            copies.append(
                pltpu.make_async_copy(
                    parts[side * NX + dx], held.at[side, dx], sems.at[side * NX + dx]
                )
            )
            copies[-1].start()
    total[...] = total_in[...]
    for copy in copies:
        copy.wait()
    x, yl, z, c = place()
    live = count_ref[0]
    hubs = held.shape[3] // NYL

    def panel(p):
        px = p // 8
        pyl = (p // 4) % 2
        dx = (x - px + NX) % NX
        slabs = []
        for k in range(4):
            pz = 2 * (p % 4) + k // 2
            dz = (z - pz + NZ) % NZ
            side = (c + k % 2) % 2
            slabs.append(held[side, dx, dz, pl.ds(pl.multiple_of(pyl * hubs, hubs), hubs), :])
        return jnp.concatenate(slabs, 0)

    def step(i, carry):
        products = []
        for u in range(UNROLL):
            t = i * UNROLL + u
            product = tile_product(tiles[t], panel(panels[0, t]))
            products.append(jnp.where(t < live, product, 0.0))
        for u in range(UNROLL):
            total[rows[0, i * UNROLL + u]] += products[u]
        return carry

    lax.fori_loop(0, (live + UNROLL - 1) // UNROLL, step, 0)

    blocks = total.shape[0]
    for b in range(blocks):
        at = pl.ds(b * 128, 128)
        v = total[b] + bias[...]
        h = filled[at, :] + v / (1.0 + jnp.exp(-v))
        hidden[at, :] = h
        q = h * h
        s = h[:, :128] + h[:, 128:]
        q = q[:, :128] + q[:, 128:]
        stats[pl.ds(b, 1), :] = jnp.sum(s.T, 0, keepdims=True)
        stats[pl.ds(blocks + b, 1), :] = jnp.sum(q.T, 0, keepdims=True)


def hub_and_hidden(count, rows, panels, tiles, total, filled, bias, parts):
    blocks, _, half = total.shape
    n = filled.shape[0]
    return pl.pallas_call(
        hub_kernel,
        out_shape=[
            jax.ShapeDtypeStruct((n, half), F32),
            jax.ShapeDtypeStruct((2 * blocks, 128), F32),
        ],
        in_specs=[SMEM, SMEM, SMEM, VMEM, VMEM, VMEM, VMEM] + [ANY] * (2 * NX),
        out_specs=[VMEM, VMEM],
        scratch_shapes=[
            pltpu.VMEM((blocks, 128, half), F32),
            pltpu.VMEM((2, NX) + parts[0].shape, F32),
            pltpu.SemaphoreType.DMA((2 * NX,)),
        ],
        name="hub_tiles",
        cost_estimate=pl.CostEstimate(
            flops=tiles.shape[0] * 128 * 128 * half * 6, bytes_accessed=16 << 20, transcendentals=0
        ),
        compiler_params=pltpu.CompilerParams(vmem_limit_bytes=32 << 20),
    )(count, rows, panels, tiles, total, filled, bias[None, :], *parts)


def norm_kernel(width, hidden, own, other, gain, out):
    blocks = own.shape[0] // 2
    sums = (own[...] + other[...]) / width
    for b in range(blocks):
        mean = jnp.broadcast_to(sums[b : b + 1], (128, 128)).T
        square = jnp.broadcast_to(sums[blocks + b : blocks + b + 1], (128, 128)).T
        scale = lax.rsqrt(square - mean * mean + 1e-05)
        at = pl.ds(b * 128, 128)
        for k in range(hidden.shape[1] // 128):
            lanes = pl.ds(k * 128, 128)
            out[at, lanes] = (hidden[at, lanes] - mean) * scale * gain[:, lanes]


def normalise(hidden, own, other, gain, width):
    def kernel(*refs):
        norm_kernel(width, *refs)

    return pl.pallas_call(
        kernel,
        out_shape=jax.ShapeDtypeStruct(hidden.shape, F32),
        in_specs=[VMEM] * 4,
        out_specs=VMEM,
        name="normalise",
        compiler_params=pltpu.CompilerParams(vmem_limit_bytes=16 << 20),
    )(hidden, own, other, gain[None, :])


def neighbours(first, last):
    doms = NX * NYL * NZ * NC
    prev = lax.ppermute(last, "dom", [(i, i + 1) for i in range(doms - 1)])
    after = lax.ppermute(first, "dom", [(i + 1, i) for i in range(doms - 1)])
    return prev, after


def shards(
    features,
    infill_mask,
    mask_token,
    local_rows,
    local_cols,
    local_tiles,
    hub_ids,
    hub_count,
    hub_rows,
    hub_panels,
    hub_tiles,
    mix_weight,
    mix_bias,
    norm_gain,
):
    rows, half = features.shape
    blocks = rows // 128
    edge = 512

    own_f = hub_rows_of(hub_ids, infill_mask, features, mask_token)
    own_g = send(own_f, lambda x, yl, z, c, f: (x, yl, z, c, 1 - f))
    other_f = send(own_f, lambda x, yl, z, c, f: (x, 1 - yl, z, c, f))
    other_g = send(own_f, lambda x, yl, z, c, f: (x, 1 - yl, z, c, 1 - f))

    filled = jnp.where(infill_mask[:, None] == 1, mask_token[None, :], features)
    filled, own_f = lax.optimization_barrier((filled, own_f))
    first, mid, last = filled[:edge], filled[edge : rows - edge], filled[rows - edge :]
    swap = lambda v: send(v, lambda x, yl, z, c, f: (x, yl, z, c, 1 - f))
    first_g, last_g, mid_g = swap(first), swap(last), swap(mid)

    y_hub = mix_hub(own_f, own_g, other_f, other_g, mix_weight)
    stack = [y_hub]
    for d in range(1, NZ):
        stack.append(send(y_hub, lambda x, yl, z, c, f: (x, yl, z + d, c, f)))
    line = jnp.stack(stack, 0)
    parts = [line]
    for d in range(1, NX):
        parts.append(send(line, lambda x, yl, z, c, f: (x + d, yl, z, c, f)))
    parts = parts + [send(v, lambda x, yl, z, c, f: (x, yl, z, 1 - c, f)) for v in parts]

    y_first = mix(first, first_g, mix_weight)
    y_last = mix(last, last_g, mix_weight)
    prev, after = neighbours(y_first, y_last)
    y_mid = mix(mid, mid_g, mix_weight)
    total = local_sum(
        local_rows, local_cols, local_tiles[0], (prev, y_first, y_mid, y_last, after), blocks
    )
    hidden, stats = hub_and_hidden(
        hub_count, hub_rows, hub_panels, hub_tiles[0], total, filled, mix_bias, parts
    )
    stats_g = swap(stats)
    return normalise(hidden, stats, stats_g, norm_gain, half * lax.axis_size("feat"))


def solution(mesh):
    in_specs = (
        P("dom", "feat"),
        P("dom"),
        P("feat"),
        P("dom", None),
        P("dom", None),
        P("dom", None, None, None),
        P("dom"),
        P("dom"),
        P("dom", None),
        P("dom", None),
        P("dom", None, None, None),
        P(None, "feat"),
        P("feat"),
        P("feat"),
    )
    out_specs = P("dom", "feat")
    return jax.shard_map(shards, mesh=mesh, in_specs=in_specs, out_specs=out_specs, check_vma=False)
```

time: 391 us -> 102 us (0.26)
  waiting for transfers between devices: 241 us -> 27.3 us
  matrix products: 58.9 us -> 0 us
  local copies, waits for them, and re-layouts: 50.7 us -> 4.08 us
  starting transfers between devices: 9.05 us -> 44.1 us
  Pallas kernels: 0 us -> 22.3 us
  between operations: 14.2 us -> 0.95 us
  blocking collectives: 9.5 us -> 0 us
  other arithmetic: 6.81 us -> 1.93 us
    all_gather x2 -> x0, waiting for transfers between devices: 214 us -> none  [the longest x1 152 us: shards(): every_hub = lax.all_gather(owned_hubs, 'dom', axis=0, tiled=True)]
    dot_general x5 -> x0, matrix products: 58.9 us -> none  [the longest x2 39.2 us: block_sum(): products = jnp.einsum('tij,tjf->tif', tiles, picked, precision=highest)]
    ppermute x2 -> x23, starting transfers between devices: 9.01 us -> 44.1 us  [the longest x21 39.9 us: send(): return lax.ppermute(value, BOTH, shift(move))]
    pallas_call x0 -> x8, Pallas kernels: none -> 22.3 us  [the longest x3 6.06 us: mix(): pl.pallas_call(mix_kernel, out_shape=jax.ShapeDtypeStruct((rows, half), F...]
    dot_general x2 -> x0, local copies, waits for them, and re-layouts: 18.5 us -> none  [block_sum(): products = jnp.einsum('tij,tjf->tif', tiles, picked, precision=highest)]
    gather x3 -> x0, local copies, waits for them, and re-layouts: 16.4 us -> none  [the longest x1 7.09 us: shards(): ext_blocks[col_ids]]
    psum x1 -> x0, blocking collectives: 9.5 us -> none  [shards(): lax.psum((jnp.sum(hidden, 1), jnp.sum(hidden * hidden, 1)), 'feat')]
    reshape x1 -> x0, local copies, waits for them, and re-layouts: 6.62 us -> none  [shards(): ext_blocks = extended.reshape(3 * blocks, 128, half)]
  transfers between devices with their start and end apart: 4 -> 23, of which waited for: 4 -> 8; matrix products, arithmetic and copies ran while one was open for 12% -> 5% of each run, Pallas kernels for 0% -> 13%
where the time goes in v1:
time: 102 us; the launch traced here: 101 us
  starting transfers between devices  44.1 us (43%)
  waiting for transfers between devices  27.3 us (27%)
  Pallas kernels  22.3 us (22%)
  local copies, waits for them, and re-layouts  4.08 us (4%)
  other arithmetic  1.93 us (2%)
    ppermute x21, starting transfers between devices, send(): return lax.ppermute(value, BOTH, shift(move))  39.9 us
    ppermute x21, waiting for transfers between devices, send(): return lax.ppermute(value, BOTH, shift(move))  27.3 us
    pallas_call x3, Pallas kernels, mix(): pl.pallas_call(mix_kernel, out_shape=jax.ShapeDtypeStruct((rows, half), F...  6.06 us
    pallas_call x1, Pallas kernels, local_sum(): pl.pallas_call(local_kernel, out_shape=jax.ShapeDtypeStruct((blocks, 128,...  5.09 us
    pallas_call x1, Pallas kernels, hub_and_hidden(): pl.pallas_call(hub_kernel, out_shape=[jax.ShapeDtypeStruct((n, half), F32...  4.08 us
    pallas_call x1, Pallas kernels, hub_rows_of(): pl.pallas_call(hub_rows_kernel, out_shape=jax.ShapeDtypeStruct((count, fe...  3.09 us
    unnamed x35, local copies, waits for them, and re-layouts  2.17 us
    ppermute x1, starting transfers between devices, neighbours(): after = lax.ppermute(first, 'dom', [(i + 1, i) for i in range(doms - 1)])  2.12 us
  transfers between devices with their start and end apart: 23, of which 8 were waited for; matrix products, arithmetic and copies ran while one was open for 5% of the time, Pallas kernels for 13%

profile of v1, /device:TPU:8, one launch (start us, length us, event | category | flops | bytes accessed | tf_op | source)
XLA Modules:
  0.0 100.7 jit_solution(10740761571753466007)
XLA Ops:
  0.0 3.1 %hub_rows.1.own_f = f32[32,256]{1,0:T(8,128)} custom-call(s32[32]{0:T(128)} %ids.1, s32[2048]{0:T(1024)} %mask.1, f32[2048,256]{1,0:T(8,128)} %features.1, f32[1,256]{1,0:T(1,128)} %bitcast.25), custom_call_target="tpu_custom_call" | custom-call | tf_op jit(solution)/shard_map/hub_rows/pallas_call | solution.py:82
  3.1 2.4 %collective-permute-start.5 = (f32[32,256]{1,0:T(8,128)}, f32[32,256]{1,0:T(8,128)S(1)}, u32[]{:S(2)}, u32[]{:S(2)}) collective-permute-start(f32[32,256]{1,0:T(8,128)} %hub_rows.1.own_f), channel_id=1, source_target_pairs={{0,1},{1,0},{2,3},{3,2},{4,5},{5,4},{6,7},{7,6},{8,9},{9,8},{10,11... | collective-permute-start | bytes 98312 | tf_op jit(solution)/shard_map/ppermute | solution.py:39
  7.3 1.9 %broadcast_select_fusion.filled = f32[2048,256]{1,0:T(8,128)S(1)} fusion(f32[2048,256]{1,0:T(8,128)} %features.1, f32[256]{0:T(256)S(1)} %copy-done.13, pred[2048]{0:T(1024)(128)(4,1)S(1)} %broadcast_compare_fusion), kind=kLoop, calls=%fused_computation | loop fusion | flops 524288 | bytes 4197376 | tf_op jit(solution)/shard_map/jit(_where)/select_n | solution.py:338
  10.1 2.3 %collective-permute-start = (f32[512,256]{1,0:T(8,128)}, f32[512,256]{1,0:T(8,128)}, u32[]{:S(2)}, u32[]{:S(2)}) collective-permute-start(f32[512,256]{1,0:T(8,128)} %get-tuple-element.14.xf), channel_id=1, source_target_pairs={{0,1},{1,0},{2,3},{3,2},{4,5},{5,4},{6,7},{7,6},{8,9},{9,8},{10,11... | collective-permute-start | bytes 1572872 | tf_op jit(solution)/shard_map/ppermute | solution.py:39
  14.7 2.3 %collective-permute-start.3 = (f32[1024,256]{1,0:T(8,128)}, f32[1024,256]{1,0:T(8,128)}, u32[]{:S(2)}, u32[]{:S(2)}) collective-permute-start(f32[1024,256]{1,0:T(8,128)} %slice.11.xf), channel_id=1, source_target_pairs={{0,1},{1,0},{2,3},{3,2},{4,5},{5,4},{6,7},{7,6},{8,9},{9,8},{10,11... | collective-permute-start | bytes 3145736 | tf_op jit(solution)/shard_map/ppermute | solution.py:39
  18.2 2.0 %mix_hub.1 = f32[64,256]{1,0:T(8,128)} custom-call(f32[32,256]{1,0:T(8,128)} %hub_rows.1.own_f, f32[32,256]{1,0:T(8,128)} %copy-done.10, f32[32,256]{1,0:T(8,128)} %copy-done.11, f32[32,256]{1,0:T(8,128)} %copy-done.12, f32[512,256]{1,0:T(8,128)} %weight.7), custom_call_target="tpu_custom_call" | custom-call | tf_op jit(solution)/shard_map/mix_hub/pallas_call | solution.py:140
  23.0 3.3 %collective-permute-start.9 = (f32[64,256]{1,0:T(8,128)}, f32[64,256]{1,0:T(8,128)S(1)}, u32[]{:S(2)}, u32[]{:S(2)}) collective-permute-start(f32[64,256]{1,0:T(8,128)} %mix_hub.1), channel_id=1, source_target_pairs={{0,8},{1,9},{2,10},{3,11},{4,12},{5,13},{6,14},{7,15},{8,16},{9,17... | collective-permute-start | bytes 196616 | tf_op jit(solution)/shard_map/ppermute | solution.py:39
  26.3 2.5 %collective-permute-done.8 = f32[64,256]{1,0:T(8,128)S(1)} collective-permute-done((f32[64,256]{1,0:T(8,128)}, f32[64,256]{1,0:T(8,128)S(1)}, u32[]{:S(2)}, u32[]{:S(2)}) %collective-permute-start.8) | collective-permute-done | bytes 65568 | tf_op jit(solution)/shard_map/ppermute | solution.py:39
  28.8 2.0 %collective-permute-start.10 = (f32[64,256]{1,0:T(8,128)}, f32[64,256]{1,0:T(8,128)S(1)}, u32[]{:S(2)}, u32[]{:S(2)}) collective-permute-start(f32[64,256]{1,0:T(8,128)} %mix_hub.1), channel_id=1, source_target_pairs={{0,12},{1,13},{2,14},{3,15},{4,16},{5,17},{6,18},{7,19},{8,20},{9,... | collective-permute-start | bytes 196616 | tf_op jit(solution)/shard_map/ppermute | solution.py:39
  30.9 6.1 %collective-permute-start.11 = (f32[64,256]{1,0:T(8,128)}, f32[64,256]{1,0:T(8,128)S(1)}, u32[]{:S(2)}, u32[]{:S(2)}) collective-permute-start(f32[64,256]{1,0:T(8,128)} %mix_hub.1), channel_id=1, source_target_pairs={{0,16},{1,17},{2,18},{3,19},{4,20},{5,21},{6,22},{7,23},{8,24},{9,... | collective-permute-start | bytes 196616 | tf_op jit(solution)/shard_map/ppermute | solution.py:39
  37.5 3.0 %collective-permute-start.12 = (f32[64,256]{1,0:T(8,128)}, f32[64,256]{1,0:T(8,128)S(1)}, u32[]{:S(2)}, u32[]{:S(2)}) collective-permute-start(f32[64,256]{1,0:T(8,128)} %mix_hub.1), channel_id=1, source_target_pairs={{0,20},{1,21},{2,22},{3,23},{4,24},{5,25},{6,26},{7,27},{8,28},{9,... | collective-permute-start | bytes 196616 | tf_op jit(solution)/shard_map/ppermute | solution.py:39
  40.6 2.3 %collective-permute-start.13 = (f32[64,256]{1,0:T(8,128)}, f32[64,256]{1,0:T(8,128)S(1)}, u32[]{:S(2)}, u32[]{:S(2)}) collective-permute-start(f32[64,256]{1,0:T(8,128)} %mix_hub.1), channel_id=1, source_target_pairs={{0,24},{1,25},{2,26},{3,27},{4,28},{5,29},{6,30},{7,31},{8,0},{9,1... | collective-permute-start | bytes 196616 | tf_op jit(solution)/shard_map/ppermute | solution.py:39
  44.1 3.6 %collective-permute-start.14 = (f32[64,256]{1,0:T(8,128)}, f32[64,256]{1,0:T(8,128)S(1)}, u32[]{:S(2)}, u32[]{:S(2)}) collective-permute-start(f32[64,256]{1,0:T(8,128)} %mix_hub.1), channel_id=1, source_target_pairs={{0,28},{1,29},{2,30},{3,31},{4,0},{5,1},{6,2},{7,3},{8,4},{9,5},{1... | collective-permute-start | bytes 196616 | tf_op jit(solution)/shard_map/ppermute | solution.py:39
  47.8 3.2 %collective-permute-done.14 = f32[64,256]{1,0:T(8,128)S(1)} collective-permute-done((f32[64,256]{1,0:T(8,128)}, f32[64,256]{1,0:T(8,128)S(1)}, u32[]{:S(2)}, u32[]{:S(2)}) %collective-permute-start.14) | collective-permute-done | bytes 65568 | tf_op jit(solution)/shard_map/ppermute | solution.py:39
  52.5 2.7 %collective-permute-start.16 = (f32[8,64,256]{2,1,0:T(8,128)S(1)}, f32[8,64,256]{2,1,0:T(8,128)S(1)}, u32[]{:S(2)}, u32[]{:S(2)}) collective-permute-start(f32[8,64,256]{2,1,0:T(8,128)S(1)} %bitcast_dynamic-update-slice_fusion.rest_0_), channel_id=1, source_target_pairs={{0,128},{1,129},{2,130},{3,131},{4,132},{5,133},{6,134},{7,135},{8... | collective-permute-start | bytes 1572872 | tf_op jit(solution)/shard_map/ppermute | solution.py:39
  58.5 2.1 %collective-permute-start.1 = (f32[512,256]{1,0:T(8,128)S(1)}, f32[512,256]{1,0:T(8,128)S(1)}, u32[]{:S(2)}, u32[]{:S(2)}) collective-permute-start(f32[512,256]{1,0:T(8,128)S(1)} %mix_rows.3.last), channel_id=1, source_target_pairs={{0,2},{2,4},{4,6},{6,8},{8,10},{10,12},{12,14},{14,16},{16,18},{18... | collective-permute-start | bytes 1572872 | tf_op jit(solution)/shard_map/ppermute | solution.py:308
  62.4 3.7 %collective-permute-done.15.rest_1_ = f32[8,64,256]{2,1,0:T(8,128)S(1)} collective-permute-done((f32[8,64,256]{2,1,0:T(8,128)S(1)}, f32[8,64,256]{2,1,0:T(8,128)S(1)}, u32[]{:S(2)}, u32[]{:S(2)}) %collective-permute-start.15) | collective-permute-done | bytes 524320 | tf_op jit(solution)/shard_map/ppermute | solution.py:39
  66.1 2.1 %collective-permute-start.4 = (f32[512,256]{1,0:T(8,128)S(1)}, f32[512,256]{1,0:T(8,128)S(1)}, u32[]{:S(2)}, u32[]{:S(2)}) collective-permute-start(f32[512,256]{1,0:T(8,128)S(1)} %mix_rows.4.first), channel_id=1, source_target_pairs={{2,0},{4,2},{6,4},{8,6},{10,8},{12,10},{14,12},{16,14},{18,16},{20... | collective-permute-start | bytes 1572872 | tf_op jit(solution)/shard_map/ppermute | solution.py:309
  68.2 11.6 %collective-permute-done.16.rest_2_ = f32[8,64,256]{2,1,0:T(8,128)S(1)} collective-permute-done((f32[8,64,256]{2,1,0:T(8,128)S(1)}, f32[8,64,256]{2,1,0:T(8,128)S(1)}, u32[]{:S(2)}, u32[]{:S(2)}) %collective-permute-start.16) | collective-permute-done | bytes 524320 | tf_op jit(solution)/shard_map/ppermute | solution.py:39
  81.5 2.5 %mix_rows.5.mid = f32[1024,256]{1,0:T(8,128)S(1)} custom-call(f32[1024,256]{1,0:T(8,128)} %slice.11.xf, f32[1024,256]{1,0:T(8,128)} %collective-permute-done.3.xg, f32[512,256]{1,0:T(8,128)S(1)} %copy-done), custom_call_target="tpu_custom_call" | custom-call | flops 805306368 | bytes 3145728 | tf_op jit(solution)/shard_map/mix_rows/pallas_call | solution.py:115
  84.1 5.1 %local_tiles.1.total_in = f32[16,128,256]{2,1,0:T(8,128)S(1)} custom-call(s32[1,64]{1,0:T(1,128)S(1)} %copy-done.5, s32[1,64]{1,0:T(1,128)S(1)} %copy-done.6, f32[64,128,128]{2,1,0:T(8,128)S(1)} %bitcast.21, f32[512,256]{1,0:T(8,128)S(1)} %collective-permute-done.1.prev, f32[512,256]{1,0:T(8,128)S(1)} %mix_rows.4.first, f32[1024,256]{1,0:T(8,128)S(1)} %mix_rows.5.mid, ...), custom_call_target="tpu_custom_call" | custom-call | flops 1610612736 | bytes 12582912 | tf_op jit(solution)/shard_map/local_tiles/pallas_call | solution.py:183
  89.3 4.1 %hub_tiles.1 = (f32[2048,256]{1,0:T(8,128)S(1)}, f32[32,128]{1,0:T(8,128)S(1)}) custom-call(s32[1]{0:T(128)S(6)} %copy.22.count_ref, s32[1,64]{1,0:T(1,128)S(1)} %copy-done.7, s32[1,64]{1,0:T(1,128)S(1)} %copy-done.8, f32[64,128,128]{2,1,0:T(8,128)S(1)} %bitcast.22, f32[16,128,256]{2,1,0:T(8,128)S(1)} %local_tiles.1.total_in, ...), custom_call_target="tpu_custom_call" | custom-call | flops 1610612736 | bytes 16777216 | tf_op jit(solution)/shard_map/hub_tiles/pallas_call | solution.py:258
  94.4 4.4 %collective-permute-done.22.refs_2_ = f32[32,128]{1,0:T(8,128)S(1)} collective-permute-done((f32[32,128]{1,0:T(8,128)S(1)}, f32[32,128]{1,0:T(8,128)S(1)}, u32[]{:S(2)}, u32[]{:S(2)}) %collective-permute-start.22) | collective-permute-done | bytes 16416 | tf_op jit(solution)/shard_map/ppermute | solution.py:39
  98.8 1.9 %normalise.1 = f32[2048,256]{1,0:T(8,128)} custom-call(f32[2048,256]{1,0:T(8,128)S(1)} %get-tuple-element.11.refs_0_, f32[32,128]{1,0:T(8,128)S(1)} %get-tuple-element.12.refs_1_, f32[32,128]{1,0:T(8,128)S(1)} %collective-permute-done.22.refs_2_, f32[1,256]{1,0:T(1,128)S(1)} %bitcast.23), custom_call_target="tpu_custom_call" | custom-call | tf_op jit(solution)/shard_map/normalise/pallas_call | solution.py:296
  (70 shorter events, 19.5 us)
Async XLA Ops:
  3.1 11.6 %collective-permute-start.5 = (f32[32,256]{1,0:T(8,128)}, f32[32,256]{1,0:T(8,128)S(1)}, u32[]{:S(2)}, u32[]{:S(2)}) collective-permute-start(f32[32,256]{1,0:T(8,128)} %hub_rows.1.own_f), channel_id=1, source_target_pairs={{0,1},{1,0},{2,3},{3,2},{4,5},{5,4},{6,7},{7,6},{8,9},{9,8},{10,11... | collective-permute-start | bytes 98312 | tf_op jit(solution)/shard_map/ppermute | solution.py:39
  5.5 11.5 %collective-permute-start.6 = (f32[32,256]{1,0:T(8,128)}, f32[32,256]{1,0:T(8,128)S(1)}, u32[]{:S(2)}, u32[]{:S(2)}) collective-permute-start(f32[32,256]{1,0:T(8,128)} %hub_rows.1.own_f), channel_id=1, source_target_pairs={{0,32},{1,33},{2,34},{3,35},{4,36},{5,37},{6,38},{7,39},{8,40},{9,... | collective-permute-start | bytes 98312 | tf_op jit(solution)/shard_map/ppermute | solution.py:39
  6.8 10.2 %collective-permute-start.7 = (f32[32,256]{1,0:T(8,128)}, f32[32,256]{1,0:T(8,128)S(1)}, u32[]{:S(2)}, u32[]{:S(2)}) collective-permute-start(f32[32,256]{1,0:T(8,128)} %hub_rows.1.own_f), channel_id=1, source_target_pairs={{0,33},{1,32},{2,35},{3,34},{4,37},{5,36},{6,39},{7,38},{8,41},{9,... | collective-permute-start | bytes 98312 | tf_op jit(solution)/shard_map/ppermute | solution.py:39
  10.1 46.6 %copy-start = (f32[512,256]{1,0:T(8,128)S(1)}, f32[512,256]{1,0:T(8,128)}, u32[]{:S(2)}) copy-start(f32[512,256]{1,0:T(8,128)} %weight.7) | copy-start | bytes 1572868
  10.1 45.2 %collective-permute-start = (f32[512,256]{1,0:T(8,128)}, f32[512,256]{1,0:T(8,128)}, u32[]{:S(2)}, u32[]{:S(2)}) collective-permute-start(f32[512,256]{1,0:T(8,128)} %get-tuple-element.14.xf), channel_id=1, source_target_pairs={{0,1},{1,0},{2,3},{3,2},{4,5},{5,4},{6,7},{7,6},{8,9},{9,8},{10,11... | collective-permute-start | bytes 1572872 | tf_op jit(solution)/shard_map/ppermute | solution.py:39
  12.4 46.1 %collective-permute-start.2 = (f32[512,256]{1,0:T(8,128)S(1)}, f32[512,256]{1,0:T(8,128)}, u32[]{:S(2)}, u32[]{:S(2)}) collective-permute-start(f32[512,256]{1,0:T(8,128)S(1)} %get-tuple-element.13.xf), channel_id=1, source_target_pairs={{0,1},{1,0},{2,3},{3,2},{4,5},{5,4},{6,7},{7,6},{8,9},{9,8},{10,11... | collective-permute-start | bytes 1572872 | tf_op jit(solution)/shard_map/ppermute | solution.py:39
  14.7 65.8 %collective-permute-start.3 = (f32[1024,256]{1,0:T(8,128)}, f32[1024,256]{1,0:T(8,128)}, u32[]{:S(2)}, u32[]{:S(2)}) collective-permute-start(f32[1024,256]{1,0:T(8,128)} %slice.11.xf), channel_id=1, source_target_pairs={{0,1},{1,0},{2,3},{3,2},{4,5},{5,4},{6,7},{7,6},{8,9},{9,8},{10,11... | collective-permute-start | bytes 3145736 | tf_op jit(solution)/shard_map/ppermute | solution.py:39
  20.2 8.5 %collective-permute-start.8 = (f32[64,256]{1,0:T(8,128)}, f32[64,256]{1,0:T(8,128)S(1)}, u32[]{:S(2)}, u32[]{:S(2)}) collective-permute-start(f32[64,256]{1,0:T(8,128)} %mix_hub.1), channel_id=1, source_target_pairs={{0,4},{1,5},{2,6},{3,7},{4,8},{5,9},{6,10},{7,11},{8,12},{9,13},{1... | collective-permute-start | bytes 196616 | tf_op jit(solution)/shard_map/ppermute | solution.py:39
  23.0 7.9 %collective-permute-start.9 = (f32[64,256]{1,0:T(8,128)}, f32[64,256]{1,0:T(8,128)S(1)}, u32[]{:S(2)}, u32[]{:S(2)}) collective-permute-start(f32[64,256]{1,0:T(8,128)} %mix_hub.1), channel_id=1, source_target_pairs={{0,8},{1,9},{2,10},{3,11},{4,12},{5,13},{6,14},{7,15},{8,16},{9,17... | collective-permute-start | bytes 196616 | tf_op jit(solution)/shard_map/ppermute | solution.py:39
  28.8 8.7 %collective-permute-start.10 = (f32[64,256]{1,0:T(8,128)}, f32[64,256]{1,0:T(8,128)S(1)}, u32[]{:S(2)}, u32[]{:S(2)}) collective-permute-start(f32[64,256]{1,0:T(8,128)} %mix_hub.1), channel_id=1, source_target_pairs={{0,12},{1,13},{2,14},{3,15},{4,16},{5,17},{6,18},{7,19},{8,20},{9,... | collective-permute-start | bytes 196616 | tf_op jit(solution)/shard_map/ppermute | solution.py:39
  30.9 9.7 %collective-permute-start.11 = (f32[64,256]{1,0:T(8,128)}, f32[64,256]{1,0:T(8,128)S(1)}, u32[]{:S(2)}, u32[]{:S(2)}) collective-permute-start(f32[64,256]{1,0:T(8,128)} %mix_hub.1), channel_id=1, source_target_pairs={{0,16},{1,17},{2,18},{3,19},{4,20},{5,21},{6,22},{7,23},{8,24},{9,... | collective-permute-start | bytes 196616 | tf_op jit(solution)/shard_map/ppermute | solution.py:39
  37.5 6.6 %collective-permute-start.12 = (f32[64,256]{1,0:T(8,128)}, f32[64,256]{1,0:T(8,128)S(1)}, u32[]{:S(2)}, u32[]{:S(2)}) collective-permute-start(f32[64,256]{1,0:T(8,128)} %mix_hub.1), channel_id=1, source_target_pairs={{0,20},{1,21},{2,22},{3,23},{4,24},{5,25},{6,26},{7,27},{8,28},{9,... | collective-permute-start | bytes 196616 | tf_op jit(solution)/shard_map/ppermute | solution.py:39
  40.6 7.2 %collective-permute-start.13 = (f32[64,256]{1,0:T(8,128)}, f32[64,256]{1,0:T(8,128)S(1)}, u32[]{:S(2)}, u32[]{:S(2)}) collective-permute-start(f32[64,256]{1,0:T(8,128)} %mix_hub.1), channel_id=1, source_target_pairs={{0,24},{1,25},{2,26},{3,27},{4,28},{5,29},{6,30},{7,31},{8,0},{9,1... | collective-permute-start | bytes 196616 | tf_op jit(solution)/shard_map/ppermute | solution.py:39
  44.1 6.9 %collective-permute-start.14 = (f32[64,256]{1,0:T(8,128)}, f32[64,256]{1,0:T(8,128)S(1)}, u32[]{:S(2)}, u32[]{:S(2)}) collective-permute-start(f32[64,256]{1,0:T(8,128)} %mix_hub.1), channel_id=1, source_target_pairs={{0,28},{1,29},{2,30},{3,31},{4,0},{5,1},{6,2},{7,3},{8,4},{9,5},{1... | collective-permute-start | bytes 196616 | tf_op jit(solution)/shard_map/ppermute | solution.py:39
  51.0 15.0 %collective-permute-start.15 = (f32[8,64,256]{2,1,0:T(8,128)S(1)}, f32[8,64,256]{2,1,0:T(8,128)S(1)}, u32[]{:S(2)}, u32[]{:S(2)}) collective-permute-start(f32[8,64,256]{2,1,0:T(8,128)S(1)} %bitcast_dynamic-update-slice_fusion.rest_0_), channel_id=1, source_target_pairs={{0,64},{1,65},{2,66},{3,67},{4,68},{5,69},{6,70},{7,71},{8,72},{9,... | collective-permute-start | bytes 1572872 | tf_op jit(solution)/shard_map/ppermute | solution.py:39
  52.5 27.3 %collective-permute-start.16 = (f32[8,64,256]{2,1,0:T(8,128)S(1)}, f32[8,64,256]{2,1,0:T(8,128)S(1)}, u32[]{:S(2)}, u32[]{:S(2)}) collective-permute-start(f32[8,64,256]{2,1,0:T(8,128)S(1)} %bitcast_dynamic-update-slice_fusion.rest_0_), channel_id=1, source_target_pairs={{0,128},{1,129},{2,130},{3,131},{4,132},{5,133},{6,134},{7,135},{8... | collective-permute-start | bytes 1572872 | tf_op jit(solution)/shard_map/ppermute | solution.py:39
  55.3 24.6 %collective-permute-start.17 = (f32[8,64,256]{2,1,0:T(8,128)S(1)}, f32[8,64,256]{2,1,0:T(8,128)S(1)}, u32[]{:S(2)}, u32[]{:S(2)}) collective-permute-start(f32[8,64,256]{2,1,0:T(8,128)S(1)} %bitcast_dynamic-update-slice_fusion.rest_0_), channel_id=1, source_target_pairs={{0,192},{1,193},{2,194},{3,195},{4,196},{5,197},{6,198},{7,199},{8... | collective-permute-start | bytes 1572872 | tf_op jit(solution)/shard_map/ppermute | solution.py:39
  58.5 21.9 %collective-permute-start.1 = (f32[512,256]{1,0:T(8,128)S(1)}, f32[512,256]{1,0:T(8,128)S(1)}, u32[]{:S(2)}, u32[]{:S(2)}) collective-permute-start(f32[512,256]{1,0:T(8,128)S(1)} %mix_rows.3.last), channel_id=1, source_target_pairs={{0,2},{2,4},{4,6},{6,8},{8,10},{10,12},{12,14},{14,16},{16,18},{18... | collective-permute-start | bytes 1572872 | tf_op jit(solution)/shard_map/ppermute | solution.py:308
  66.1 18.0 %collective-permute-start.4 = (f32[512,256]{1,0:T(8,128)S(1)}, f32[512,256]{1,0:T(8,128)S(1)}, u32[]{:S(2)}, u32[]{:S(2)}) collective-permute-start(f32[512,256]{1,0:T(8,128)S(1)} %mix_rows.4.first), channel_id=1, source_target_pairs={{2,0},{4,2},{6,4},{8,6},{10,8},{12,10},{14,12},{16,14},{18,16},{20... | collective-permute-start | bytes 1572872 | tf_op jit(solution)/shard_map/ppermute | solution.py:309
  79.8 9.4 %collective-permute-start.18 = (f32[8,64,256]{2,1,0:T(8,128)S(1)}, f32[8,64,256]{2,1,0:T(8,128)S(1)}, u32[]{:S(2)}, u32[]{:S(2)}) collective-permute-start(f32[8,64,256]{2,1,0:T(8,128)S(1)} %bitcast_dynamic-update-slice_fusion.rest_0_), channel_id=1, source_target_pairs={{0,2},{1,3},{2,0},{3,1},{4,6},{5,7},{6,4},{7,5},{8,10},{9,11},{10,... | collective-permute-start | bytes 1572872 | tf_op jit(solution)/shard_map/ppermute | solution.py:39
  79.8 9.4 %collective-permute-start.19 = (f32[8,64,256]{2,1,0:T(8,128)S(1)}, f32[8,64,256]{2,1,0:T(8,128)S(1)}, u32[]{:S(2)}, u32[]{:S(2)}) collective-permute-start(f32[8,64,256]{2,1,0:T(8,128)S(1)} %collective-permute-done.15.rest_1_), channel_id=1, source_target_pairs={{0,2},{1,3},{2,0},{3,1},{4,6},{5,7},{6,4},{7,5},{8,10},{9,11},{10,... | collective-permute-start | bytes 1572872 | tf_op jit(solution)/shard_map/ppermute | solution.py:39
  80.4 8.9 %collective-permute-start.20 = (f32[8,64,256]{2,1,0:T(8,128)S(1)}, f32[8,64,256]{2,1,0:T(8,128)S(1)}, u32[]{:S(2)}, u32[]{:S(2)}) collective-permute-start(f32[8,64,256]{2,1,0:T(8,128)S(1)} %collective-permute-done.16.rest_2_), channel_id=1, source_target_pairs={{0,2},{1,3},{2,0},{3,1},{4,6},{5,7},{6,4},{7,5},{8,10},{9,11},{10,... | collective-permute-start | bytes 1572872 | tf_op jit(solution)/shard_map/ppermute | solution.py:39
  80.5 8.8 %collective-permute-start.21 = (f32[8,64,256]{2,1,0:T(8,128)S(1)}, f32[8,64,256]{2,1,0:T(8,128)S(1)}, u32[]{:S(2)}, u32[]{:S(2)}) collective-permute-start(f32[8,64,256]{2,1,0:T(8,128)S(1)} %collective-permute-done.17.rest_3_), channel_id=1, source_target_pairs={{0,2},{1,3},{2,0},{3,1},{4,6},{5,7},{6,4},{7,5},{8,10},{9,11},{10,... | collective-permute-start | bytes 1572872 | tf_op jit(solution)/shard_map/ppermute | solution.py:39
  93.4 5.3 %collective-permute-start.22 = (f32[32,128]{1,0:T(8,128)S(1)}, f32[32,128]{1,0:T(8,128)S(1)}, u32[]{:S(2)}, u32[]{:S(2)}) collective-permute-start(f32[32,128]{1,0:T(8,128)S(1)} %get-tuple-element.12.refs_1_), channel_id=1, source_target_pairs={{0,1},{1,0},{2,3},{3,2},{4,5},{5,4},{6,7},{7,6},{8,9},{9,8},{10,11... | collective-permute-start | bytes 49160 | tf_op jit(solution)/shard_map/ppermute | solution.py:39
  (13 other events, 115.1 us)

commit v2 on v1

v2 whole, which is shorter than its diff:
```python
import functools

import jax
import jax.numpy as jnp
from jax import lax
from jax.experimental import pallas as pl
from jax.experimental.pallas import tpu as pltpu
from jax.sharding import PartitionSpec as P

NX, NYL, NZ, NC = 4, 2, 8, 2
BOTH = ("dom", "feat")
F32 = jnp.float32
BF = jnp.bfloat16
SMEM = pl.BlockSpec(memory_space=pltpu.SMEM)
VMEM = pl.BlockSpec(memory_space=pltpu.VMEM)
ANY = pl.BlockSpec(memory_space=pl.ANY)
LIGHT = pl.CostEstimate(flops=1, bytes_accessed=1, transcendentals=0)


def dom_index(x, yl, z, c):
    return ((x * NYL + yl) * NZ + z) * NC + c


def shift(move):
    pairs = []
    for x in range(NX):
        for yl in range(NYL):
            for z in range(NZ):
                for c in range(NC):
                    for f in range(2):
                        tx, tyl, tz, tc, tf = move(x, yl, z, c, f)
                        pairs.append(
                            (
                                dom_index(x, yl, z, c) * 2 + f,
                                dom_index(tx % NX, tyl, tz % NZ, tc) * 2 + tf,
                            )
                        )
    return pairs


def send(value, move):
    return lax.ppermute(value, BOTH, shift(move))


def place():
    dom = lax.axis_index("dom")
    c = dom % NC
    z = (dom // NC) % NZ
    yl = (dom // (NC * NZ)) % NYL
    x = dom // (NC * NZ * NYL)
    return x, yl, z, c


def split(a):
    hi = a.astype(BF)
    return hi, (a - hi.astype(F32)).astype(BF)


def dot(a, b):
    return jnp.dot(a, b, preferred_element_type=F32)


def hub_rows_kernel(ids, mask, features, token, out, sems):
    first = lax.axis_index("dom") * features.shape[0]
    count = ids.shape[0]
    copies = []
    for i in range(count):
        row = ids[i] - first
        copies.append(
            pltpu.make_async_copy(features.at[pl.ds(row, 1)], out.at[pl.ds(i, 1)], sems.at[i])
        )
        copies[-1].start()
    out[pl.ds(count, 8), :] = jnp.broadcast_to(token[...], (8, token.shape[1]))
    for i in range(count):
        copies[i].wait()
    for i in range(count):
        row = ids[i] - first
        here = pl.ds(i, 1)
        out[here, :] = jnp.where(mask[row] == 1, token[...], out[here, :])


def hub_rows_of(hub_ids, infill_mask, features, mask_token):
    count = hub_ids.shape[0]
    half = features.shape[1]
    return pl.pallas_call(
        hub_rows_kernel,
        out_shape=jax.ShapeDtypeStruct((count + 8, half), F32),
        in_specs=[SMEM, SMEM, ANY, VMEM],
        out_specs=VMEM,
        scratch_shapes=[pltpu.SemaphoreType.DMA((count,))],
        name="hub_rows",
        cost_estimate=LIGHT,
    )(hub_ids, infill_mask, features, mask_token[None, :])


def mix_rows(xf, xg, weight):
    f = lax.axis_index("feat")
    half = xf.shape[1]
    wf = weight[pl.ds(pl.multiple_of(f * half, half), half), :]
    wg = weight[pl.ds(pl.multiple_of((1 - f) * half, half), half), :]
    wfh, wfl = split(wf)
    wgh, wgl = split(wg)
    right = jnp.concatenate([wfh, wfl, wfh, wgh, wgl, wgh], 0)
    fh, fl = split(xf)
    gh, gl = split(xg)
    left = jnp.concatenate([fh, fh, fl, gh, gh, gl], 1)
    return dot(left, right)


def chosen(y, mask_row, token_y):
    here = jnp.broadcast_to(mask_row, (128, 128)).T
    halves = []
    for k in range(y.shape[1] // 128):
        lanes = slice(k * 128, (k + 1) * 128)
        halves.append(jnp.where(here == 1.0, token_y[:, lanes], y[:, lanes]))
    return jnp.concatenate(halves, 1)


def mix_into(xf, xg, weight, mask, token_y, store):
    step = 256
    for i in range(xf.shape[0] // step):
        at = pl.ds(i * step, step)
        y = mix_rows(xf[at, :], xg[at, :], weight)
        for j in range(step // 128):
            b = i * (step // 128) + j
            store(b, chosen(y[j * 128 : (j + 1) * 128], mask[b : b + 1, :], token_y[:1, :]))


def mix_kernel(xf, xg, weight, mask, token_y, *outs):
    def store(b, y):
        for out in outs:
            n = out.shape[0] // 128
            if 0 <= b < n:
                out[pl.ds(b * 128, 128), :] = y
            b -= n

    mix_into(xf, xg, weight, mask[...].astype(F32), token_y, store)


def mix(xf, xg, weight, mask, token_y, sizes):
    rows, half = xf.shape
    return pl.pallas_call(
        mix_kernel,
        out_shape=[jax.ShapeDtypeStruct((size, half), F32) for size in sizes],
        in_specs=[VMEM] * 5,
        out_specs=[VMEM] * len(sizes),
        name="mix_rows",
        cost_estimate=LIGHT,
        compiler_params=pltpu.CompilerParams(vmem_limit_bytes=16 << 20),
    )(xf, xg, weight, mask, token_y)


def mix_hub_kernel(own_f, own_g, other_f, other_g, weight, out, token_y):
    count = own_f.shape[0] - 8
    yl = place()[1]
    xf = jnp.concatenate([own_f[...], other_f[:count]], 0)
    xg = jnp.concatenate([own_g[...], other_g[:count]], 0)
    y = mix_rows(xf, xg, weight)
    out[pl.ds(pl.multiple_of(yl * count, count), count), :] = y[:count]
    token_y[...] = y[count : count + 8]
    out[pl.ds(pl.multiple_of((1 - yl) * count, count), count), :] = y[count + 8 :]


def mix_hub(own_f, own_g, other_f, other_g, weight):
    count, half = own_f.shape[0] - 8, own_f.shape[1]
    return pl.pallas_call(
        mix_hub_kernel,
        out_shape=[
            jax.ShapeDtypeStruct((2 * count, half), F32),
            jax.ShapeDtypeStruct((8, half), F32),
        ],
        in_specs=[VMEM] * 5,
        out_specs=[VMEM, VMEM],
        name="mix_hub",
        cost_estimate=LIGHT,
    )(own_f, own_g, other_f, other_g, weight)


def tile_product(tile, y):
    ah, al = split(tile)
    yh, yl = split(y)
    return dot(jnp.concatenate([ah, ah, al], 1), jnp.concatenate([yh, yl, yh], 0))


UNROLL = 8


def gathered_sum(count, index, row_of, tile_of, y_of, total):
    def step(i, carry):
        products, rows = [], []
        for u in range(UNROLL):
            k = i * UNROLL + u
            t = index(k)
            product = tile_product(tile_of(t), y_of(t))
            products.append(jnp.where(k < count, product, 0.0))
            rows.append(row_of(t))
        for u in range(UNROLL):
            total[rows[u]] += products[u]
        return carry

    lax.fori_loop(0, (count + UNROLL - 1) // UNROLL, step, 0)


def list_tiles(cols, wanted, listed):
    def clear(t, carry):
        listed[t] = 0
        return carry

    def step(t, n):
        listed[n] = t
        return n + jnp.where(wanted(cols[0, t]), 1, 0)

    lax.fori_loop(0, listed.shape[0], clear, 0)
    return lax.fori_loop(0, cols.shape[1], step, 0)


def inside(col, low, high):
    return jnp.logical_and(col >= low, col < high)


def fill_blocks(ext, at, parts):
    for part in parts:
        n = part.shape[0] // 128
        ext[pl.ds(at, n)] = part[...].reshape(n, 128, part.shape[1])
        at += n


def early_kernel(late, rows, cols, tiles, *rest):
    parts, (total, ext, listed) = rest[:-3], rest[-3:]
    total[...] = jnp.zeros_like(total)
    low, high = late
    blocks = total.shape[0]
    fill_blocks(ext, 0, parts)

    def wanted(col):
        return jnp.logical_or(inside(col, blocks, low), inside(col, high, 2 * blocks))

    def y_of(t):
        col = cols[0, t]
        at = col - blocks - jnp.where(col >= high, high - low, 0)
        return ext[jnp.clip(at, 0, ext.shape[0] - 1)]

    count = list_tiles(cols, wanted, listed)
    gathered_sum(
        count, lambda k: listed[k], lambda t: rows[0, t], lambda t: tiles[t], y_of, total
    )


def early_sum(late, rows, cols, tiles, parts, blocks):
    half = parts[0].shape[1]
    depth = sum(p.shape[0] for p in parts) // 128
    count = tiles.shape[0]
    return pl.pallas_call(
        functools.partial(early_kernel, late),
        out_shape=jax.ShapeDtypeStruct((blocks, 128, half), F32),
        in_specs=[SMEM, SMEM] + [VMEM] * (1 + len(parts)),
        out_specs=VMEM,
        scratch_shapes=[
            pltpu.VMEM((depth, 128, half), F32),
            pltpu.SMEM((count + UNROLL,), jnp.int32),
        ],
        name="early_tiles",
        cost_estimate=LIGHT,
        compiler_params=pltpu.CompilerParams(vmem_limit_bytes=24 << 20),
    )(rows, cols, tiles, *parts)


def late_kernel(
    late, rows, cols, tiles, prev, after, xf, xg, weight, mask, token_y, total_in, total, ext, listed
):
    total[...] = total_in[...]
    low, high = late
    marks = mask[...].astype(F32)
    blocks = total.shape[0]
    size = high - low
    reach = prev.shape[0] // 128
    fill_blocks(ext, size, (prev, after))

    def store(b, y):
        ext[b] = y

    mix_into(xf, xg, weight, marks[low - blocks : high - blocks], token_y, store)

    def wanted(col):
        return jnp.logical_or(
            inside(col, low, high), jnp.logical_or(col < blocks, col >= 2 * blocks)
        )

    def y_of(t):
        col = cols[0, t]
        at = jnp.where(
            col < blocks,
            size + col - (blocks - reach),
            jnp.where(col >= 2 * blocks, size + reach + col - 2 * blocks, col - low),
        )
        return ext[jnp.clip(at, 0, ext.shape[0] - 1)]

    count = list_tiles(cols, wanted, listed)
    gathered_sum(
        count, lambda k: listed[k], lambda t: rows[0, t], lambda t: tiles[t], y_of, total
    )


def late_sum(late, rows, cols, tiles, prev, after, xf, xg, weight, mask, token_y, total):
    half = xf.shape[1]
    count = tiles.shape[0]
    depth = late[1] - late[0] + (prev.shape[0] + after.shape[0]) // 128
    return pl.pallas_call(
        functools.partial(late_kernel, late),
        out_shape=jax.ShapeDtypeStruct(total.shape, F32),
        in_specs=[SMEM, SMEM] + [VMEM] * 9,
        out_specs=VMEM,
        scratch_shapes=[
            pltpu.VMEM((depth, 128, half), F32),
            pltpu.SMEM((count + UNROLL,), jnp.int32),
        ],
        name="late_tiles",
        cost_estimate=LIGHT,
        compiler_params=pltpu.CompilerParams(vmem_limit_bytes=24 << 20),
    )(rows, cols, tiles, prev, after, xf, xg, weight, mask, token_y, total)


PART_AT = (0, 2, 3, 4, 6)


def final_kernel(
    live_ref, hub_rows, panels, hub_tiles, mask, token, total_in, features, bias, *rest
):
    parts = rest[:-5]
    hidden, stats, total, held, sems = rest[-5:]
    copies = []
    for k, (part, at) in enumerate(zip(parts, PART_AT)):
        to = held.at[pl.ds(at, 2)] if len(part.shape) == 3 else held.at[at]
        copies.append(pltpu.make_async_copy(part, to, sems.at[k]))
        copies[-1].start()
    total[...] = total_in[...]
    marks = mask[...].astype(F32)
    blocks = total.shape[0]
    for copy in copies:
        copy.wait()
    x, yl, z, c = place()
    hubs = 32

    def panel(t):
        p = panels[0, t]
        px = p // 8
        pyl = (p // 4) % 2
        kx = (px - x + NX) % NX
        slabs = []
        for k in range(4):
            pz = 2 * (p % 4) + k // 2
            pc = k % 2
            kind = (pz - z + NZ) % 4
            offset = jnp.where(kind < 2, kind, kind - 4)
            far = ((pz - z - offset + 2 * NZ) % NZ) // 4
            unit = jnp.where(kind == 0, 0, jnp.where(kind == 3, 1, kind + 1))
            unit = jnp.where(kind == 2, 3, unit)
            holder = jnp.where(kx == 3, 0, 1)
            other = 4 + jnp.where(holder == c, 0, 2) + jnp.where(holder == pc, 0, 1)
            slot = jnp.where(kx % 2 == 1, other, kx + (pc + c) % 2)
            row = unit * 128 + far * 64 + pyl * hubs
            slabs.append(held[slot, pl.ds(pl.multiple_of(row, hubs), hubs), :])
        return jnp.concatenate(slabs, 0)

    gathered_sum(
        live_ref[0],
        lambda k: k,
        lambda t: hub_rows[0, t],
        lambda t: hub_tiles[t],
        panel,
        total,
    )
    for b in range(blocks):
        at = pl.ds(b * 128, 128)
        v = total[b] + bias[...]
        filled = chosen(features[at, :], marks[b : b + 1, :], token[...])
        h = filled + v / (1.0 + jnp.exp(-v))
        hidden[at, :] = h
        q = h * h
        s = h[:, :128] + h[:, 128:]
        q = q[:, :128] + q[:, 128:]
        stats[pl.ds(b, 1), :] = jnp.sum(s.T, 0, keepdims=True)
        stats[pl.ds(blocks + b, 1), :] = jnp.sum(q.T, 0, keepdims=True)


def final(scalars, arrays, parts):
    total, features = arrays[3], arrays[4]
    blocks, _, half = total.shape
    n = features.shape[0]
    return pl.pallas_call(
        final_kernel,
        out_shape=[
            jax.ShapeDtypeStruct((n, half), F32),
            jax.ShapeDtypeStruct((2 * blocks, 128), F32),
        ],
        in_specs=[SMEM] * len(scalars) + [VMEM] * len(arrays) + [ANY] * len(parts),
        out_specs=[VMEM, VMEM],
        scratch_shapes=[
            pltpu.VMEM((blocks, 128, half), F32),
            pltpu.VMEM((2 * NX,) + parts[1].shape, F32),
            pltpu.SemaphoreType.DMA((len(parts),)),
        ],
        name="final_tiles",
        cost_estimate=LIGHT,
        compiler_params=pltpu.CompilerParams(vmem_limit_bytes=32 << 20),
    )(*scalars, *arrays, *parts)


def norm_kernel(width, hidden, own, other, gain, out):
    blocks = own.shape[0] // 2
    sums = (own[...] + other[...]) / width
    for b in range(blocks):
        mean = jnp.broadcast_to(sums[b : b + 1], (128, 128)).T
        square = jnp.broadcast_to(sums[blocks + b : blocks + b + 1], (128, 128)).T
        scale = lax.rsqrt(square - mean * mean + 1e-05)
        at = pl.ds(b * 128, 128)
        for k in range(hidden.shape[1] // 128):
            lanes = pl.ds(k * 128, 128)
            out[at, lanes] = (hidden[at, lanes] - mean) * scale * gain[:, lanes]


def normalise(hidden, own, other, gain, width):
    def kernel(*refs):
        norm_kernel(width, *refs)

    return pl.pallas_call(
        kernel,
        out_shape=jax.ShapeDtypeStruct(hidden.shape, F32),
        in_specs=[VMEM] * 4,
        out_specs=VMEM,
        name="normalise",
        cost_estimate=LIGHT,
        compiler_params=pltpu.CompilerParams(vmem_limit_bytes=16 << 20),
    )(hidden, own, other, gain[None, :])


def neighbours(first, last):
    doms = NX * NYL * NZ * NC
    prev = lax.ppermute(last, "dom", [(i, i + 1) for i in range(doms - 1)])
    after = lax.ppermute(first, "dom", [(i + 1, i) for i in range(doms - 1)])
    return prev, after


def shards(
    features,
    infill_mask,
    mask_token,
    local_rows,
    local_cols,
    local_tiles,
    hub_ids,
    hub_count,
    hub_rows,
    hub_panels,
    hub_tiles,
    mix_weight,
    mix_bias,
    norm_gain,
):
    rows, half = features.shape
    blocks = rows // 128
    edge = 512
    wide = 640
    inner = wide - edge
    bounds = (((0, wide), (rows - wide, wide)), ((wide, rows - 2 * wide),))
    mask = infill_mask.reshape(blocks, 128)
    swap = lambda v: send(v, lambda x, yl, z, c, f: (x, yl, z, c, 1 - f))

    own_f = hub_rows_of(hub_ids, infill_mask, features, mask_token)
    own_g = swap(own_f)
    other_f = send(own_f, lambda x, yl, z, c, f: (x, 1 - yl, z, c, f))
    other_g = send(own_f, lambda x, yl, z, c, f: (x, 1 - yl, z, c, 1 - f))
    chunks = [
        jnp.concatenate([features[low : low + size] for low, size in ranges], 0)
        for ranges in bounds
    ]
    chunks, own_g, other_f, other_g = lax.optimization_barrier((chunks, own_g, other_f, other_g))
    chunks_g = [swap(v) for v in chunks]

    y_hub, token_y = mix_hub(own_f, own_g, other_f, other_g, mix_weight)
    own = jnp.concatenate([y_hub, send(y_hub, lambda x, yl, z, c, f: (x, yl, z + 4, c, f))], 0)
    units = [own] + [
        send(own, lambda x, yl, z, c, f: (x, yl, z + d, c, f)) for d in (1, -1, 2)
    ]
    line = jnp.concatenate(units, 0)
    sibling = lambda v: send(v, lambda x, yl, z, c, f: (x, yl, z, 1 - c, f))
    across = send(line, lambda x, yl, z, c, f: (x + 2, yl, z, c, f))
    line_s, chunks_g[0], = lax.optimization_barrier((sibling(line), chunks_g[0]))
    pair = jnp.stack([line, line_s], 0)
    beside = send(pair, lambda x, yl, z, c, f: (x + 1 - 2 * c, yl, z, c, f))

    marks = jnp.concatenate(
        [mask[low // 128 : (low + size) // 128] for low, size in bounds[0]], 0
    )
    y_first, y_left, y_right, y_last = mix(
        chunks[0], chunks_g[0], mix_weight, marks, token_y, (edge, inner, inner, edge)
    )
    prev, after = neighbours(y_first, y_last)
    late = (blocks + wide // 128, 2 * blocks - wide // 128)
    total = early_sum(
        late,
        local_rows,
        local_cols,
        local_tiles[0],
        (y_first, y_left, y_right, y_last),
        blocks,
    )
    across, beside, total, chunks_g[1], prev, after = lax.optimization_barrier(
        (across, beside, total, chunks_g[1], prev, after)
    )
    parts = (pair, across, sibling(across), beside, sibling(beside))
    total = late_sum(
        late,
        local_rows,
        local_cols,
        local_tiles[0],
        prev,
        after,
        chunks[1],
        chunks_g[1],
        mix_weight,
        mask,
        token_y,
        total,
    )
    hidden, stats = final(
        (hub_count, hub_rows, hub_panels),
        (hub_tiles[0], mask, mask_token[None, :], total, features, mix_bias[None, :]),
        parts,
    )
    return normalise(hidden, stats, swap(stats), norm_gain, half * lax.axis_size("feat"))


def solution(mesh):
    in_specs = (
        P("dom", "feat"),
        P("dom"),
        P("feat"),
        P("dom", None),
        P("dom", None),
        P("dom", None, None, None),
        P("dom"),
        P("dom"),
        P("dom", None),
        P("dom", None),
        P("dom", None, None, None),
        P(None, "feat"),
        P("feat"),
        P("feat"),
    )
    out_specs = P("dom", "feat")
    return jax.shard_map(shards, mesh=mesh, in_specs=in_specs, out_specs=out_specs, check_vma=False)
```

time: 102 us -> 97 us (0.951); the launches traced: 101 us -> 97.4 us
  starting transfers between devices: 44.1 us -> 32.1 us
  waiting for transfers between devices: 27.3 us -> 35.8 us
  Pallas kernels: 22.3 us -> 26.3 us
  local copies, waits for them, and re-layouts: 4.08 us -> 2.03 us
  other arithmetic: 1.93 us -> 0.17 us
    ppermute x21 -> x15, starting transfers between devices: 39.9 us -> 24.4 us  [send(): return lax.ppermute(value, BOTH, shift(move))]
    ppermute x21 -> x15, waiting for transfers between devices: 27.3 us -> 35.8 us  [send(): return lax.ppermute(value, BOTH, shift(move))]
    pallas_call x7 -> x6, Pallas kernels: 20.3 us -> 24.4 us  [the longest x1 7.83 us: final(): pl.pallas_call(final_kernel, out_shape=[jax.ShapeDtypeStruct((n, half), F...]
    ppermute x1, starting transfers between devices: 2.12 us -> 5.75 us  [neighbours(): after = lax.ppermute(first, 'dom', [(i + 1, i) for i in range(doms - 1)])]
    select_n x1 -> x0, other arithmetic: 1.93 us -> none  [shards(): filled = jnp.where(infill_mask[:, None] == 1, mask_token[None, :], features)]
    unnamed x35 -> x37, local copies, waits for them, and re-layouts: 2.17 us -> 0.99 us
  transfers between devices with their start and end apart: 23 -> 17, of which waited for: 8 -> 10; matrix products, arithmetic and copies ran while one was open for 5% -> 2% of each run, Pallas kernels for 13% -> 14%
where the time goes in v2:
time: 97 us; the launch traced here: 97.4 us
  waiting for transfers between devices  35.8 us (37%)
  starting transfers between devices  32.1 us (33%)
  Pallas kernels  26.3 us (27%)
  local copies, waits for them, and re-layouts  2.03 us (2%)
    ppermute x15, waiting for transfers between devices, send(): return lax.ppermute(value, BOTH, shift(move))  35.8 us
    ppermute x15, starting transfers between devices, send(): return lax.ppermute(value, BOTH, shift(move))  24.4 us
    pallas_call x1, Pallas kernels, final(): pl.pallas_call(final_kernel, out_shape=[jax.ShapeDtypeStruct((n, half), F...  7.83 us
    ppermute x1, starting transfers between devices, neighbours(): after = lax.ppermute(first, 'dom', [(i + 1, i) for i in range(doms - 1)])  5.75 us
    pallas_call x1, Pallas kernels, late_sum(): pl.pallas_call(functools.partial(late_kernel, late), out_shape=jax.ShapeD...  5.21 us
    pallas_call x1, Pallas kernels, early_sum(): pl.pallas_call(functools.partial(early_kernel, late), out_shape=jax.Shape...  3.9 us
    pallas_call x1, Pallas kernels, hub_rows_of(): pl.pallas_call(hub_rows_kernel, out_shape=jax.ShapeDtypeStruct((count + 8...  2.81 us
    pallas_call x1, Pallas kernels, mix(): pl.pallas_call(mix_kernel, out_shape=[jax.ShapeDtypeStruct((size, half),...  2.6 us
  transfers between devices with their start and end apart: 17, of which 10 were waited for; matrix products, arithmetic and copies ran while one was open for 2% of the time, Pallas kernels for 14%

profile of v2, /device:TPU:8, one launch (start us, length us, event | category | flops | bytes accessed | tf_op | source)
XLA Modules:
  0.0 97.4 jit_solution(3714076093249433532)
XLA Ops:
  0.0 2.8 %hub_rows.2.own_f = f32[40,256]{1,0:T(8,128)} custom-call(s32[32]{0:T(128)} %ids.1, s32[2048]{0:T(1024)} %mask.1, f32[2048,256]{1,0:T(8,128)} %features.3, f32[1,256]{1,0:T(1,128)} %bitcast.17), custom_call_target="tpu_custom_call" | custom-call | flops 1 | bytes 1 | tf_op jit(solution)/shard_map/hub_rows/pallas_call | solution.py:85
  2.8 2.4 %collective-permute-start = (f32[40,256]{1,0:T(8,128)}, f32[40,256]{1,0:T(8,128)S(1)}, u32[]{:S(2)}, u32[]{:S(2)}) collective-permute-start(f32[40,256]{1,0:T(8,128)} %hub_rows.2.own_f), channel_id=1, source_target_pairs={{0,1},{1,0},{2,3},{3,2},{4,5},{5,4},{6,7},{7,6},{8,9},{9,8},{10,11... | collective-permute-start | bytes 122888 | tf_op jit(solution)/shard_map/ppermute | solution.py:42
  5.2 1.3 %collective-permute-start.1 = (f32[40,256]{1,0:T(8,128)}, f32[40,256]{1,0:T(8,128)S(1)}, u32[]{:S(2)}, u32[]{:S(2)}) collective-permute-start(f32[40,256]{1,0:T(8,128)} %hub_rows.2.own_f), channel_id=1, source_target_pairs={{0,32},{1,33},{2,34},{3,35},{4,36},{5,37},{6,38},{7,39},{8,40},{9,... | collective-permute-start | bytes 122888 | tf_op jit(solution)/shard_map/ppermute | solution.py:42
  9.4 1.3 %collective-permute-done.2.other_g = f32[40,256]{1,0:T(8,128)S(1)} collective-permute-done((f32[40,256]{1,0:T(8,128)}, f32[40,256]{1,0:T(8,128)S(1)}, u32[]{:S(2)}, u32[]{:S(2)}) %collective-permute-start.2) | collective-permute-done | bytes 40992 | tf_op jit(solution)/shard_map/ppermute | solution.py:42
  10.8 2.7 %collective-permute-start.9 = (f32[1280,256]{1,0:T(8,128)S(1)}, f32[1280,256]{1,0:T(8,128)}, u32[]{:S(2)}, u32[]{:S(2)}) collective-permute-start(f32[1280,256]{1,0:T(8,128)S(1)} %pad_maximum_fusion.xf), channel_id=1, source_target_pairs={{0,1},{1,0},{2,3},{3,2},{4,5},{5,4},{6,7},{7,6},{8,9},{9,8},{10,11... | collective-permute-start | bytes 3932168 | tf_op jit(solution)/shard_map/ppermute | solution.py:42
  13.5 2.1 %mix_hub.1 = (f32[64,256]{1,0:T(8,128)}, f32[8,256]{1,0:T(8,128)}) custom-call(f32[40,256]{1,0:T(8,128)} %hub_rows.2.own_f, f32[40,256]{1,0:T(8,128)} %copy-done.14, f32[40,256]{1,0:T(8,128)} %copy-done.15, f32[40,256]{1,0:T(8,128)} %copy-done.16, f32[512,256]{1,0:T(8,128)} %weight.5), custom_call_target="tpu_custom_call" | custom-call | flops 1 | bytes 1 | tf_op jit(solution)/shard_map/mix_hub/pallas_call | solution.py:166
  15.5 5.7 %collective-permute-start.3 = (f32[64,256]{1,0:T(8,128)}, f32[64,256]{1,0:T(8,128)S(1)}, u32[]{:S(2)}, u32[]{:S(2)}) collective-permute-start(f32[64,256]{1,0:T(8,128)} %get-tuple-element.29), channel_id=1, source_target_pairs={{0,16},{1,17},{2,18},{3,19},{4,20},{5,21},{6,22},{7,23},{8,24},{9,... | collective-permute-start | bytes 196616 | tf_op jit(solution)/shard_map/ppermute | solution.py:42
  22.1 1.9 %collective-permute-done.3 = f32[64,256]{1,0:T(8,128)S(1)} collective-permute-done((f32[64,256]{1,0:T(8,128)}, f32[64,256]{1,0:T(8,128)S(1)}, u32[]{:S(2)}, u32[]{:S(2)}) %collective-permute-start.3) | collective-permute-done | bytes 65568 | tf_op jit(solution)/shard_map/ppermute | solution.py:42
  25.0 3.6 %collective-permute-start.5 = (f32[128,256]{1,0:T(8,128)S(1)}, f32[128,256]{1,0:T(8,128)S(1)}, u32[]{:S(2)}, u32[]{:S(2)}) collective-permute-start(f32[128,256]{1,0:T(8,128)S(1)} %get-tuple-element.49), channel_id=1, source_target_pairs={{0,28},{1,29},{2,30},{3,31},{4,0},{5,1},{6,2},{7,3},{8,4},{9,5},{1... | collective-permute-start | bytes 393224 | tf_op jit(solution)/shard_map/ppermute | solution.py:42
  28.6 4.2 %collective-permute-done.4 = f32[128,256]{1,0:T(8,128)S(1)} collective-permute-done((f32[128,256]{1,0:T(8,128)S(1)}, f32[128,256]{1,0:T(8,128)S(1)}, u32[]{:S(2)}, u32[]{:S(2)}) %collective-permute-start.4) | collective-permute-done | bytes 131104 | tf_op jit(solution)/shard_map/ppermute | solution.py:42
  32.8 3.7 %collective-permute-done.6 = f32[128,256]{1,0:T(8,128)S(1)} collective-permute-done((f32[128,256]{1,0:T(8,128)S(1)}, f32[128,256]{1,0:T(8,128)S(1)}, u32[]{:S(2)}, u32[]{:S(2)}) %collective-permute-start.6) | collective-permute-done | bytes 131104 | tf_op jit(solution)/shard_map/ppermute | solution.py:42
  36.6 1.9 %collective-permute-done.8 = f32[512,256]{1,0:T(8,128)S(1)} collective-permute-done((f32[512,256]{1,0:T(8,128)S(1)}, f32[512,256]{1,0:T(8,128)S(1)}, u32[]{:S(2)}, u32[]{:S(2)}) %collective-permute-start.8) | collective-permute-done | bytes 524320 | tf_op jit(solution)/shard_map/ppermute | solution.py:42
  38.5 2.9 %collective-permute-done.9.xg = f32[1280,256]{1,0:T(8,128)} collective-permute-done((f32[1280,256]{1,0:T(8,128)S(1)}, f32[1280,256]{1,0:T(8,128)}, u32[]{:S(2)}, u32[]{:S(2)}) %collective-permute-start.9) | collective-permute-done | bytes 1310752 | tf_op jit(solution)/shard_map/ppermute | solution.py:42
  41.6 1.6 %collective-permute-start.10 = (f32[2,512,256]{2,1,0:T(8,128)S(1)}, f32[2,512,256]{2,1,0:T(8,128)S(1)}, u32[]{:S(2)}, u32[]{:S(2)}) collective-permute-start(f32[2,512,256]{2,1,0:T(8,128)S(1)} %pad_maximum_fusion.1.rest_0_), channel_id=1, source_target_pairs={{0,64},{1,65},{2,194},{3,195},{4,68},{5,69},{6,198},{7,199},{8,72}... | collective-permute-start | bytes 3145736 | tf_op jit(solution)/shard_map/ppermute | solution.py:42
  44.3 2.8 %collective-permute-start.7 = (f32[512,256]{1,0:T(8,128)S(1)}, f32[512,256]{1,0:T(8,128)S(1)}, u32[]{:S(2)}, u32[]{:S(2)}) collective-permute-start(f32[512,256]{1,0:T(8,128)S(1)} %constant_dynamic-update-slice_fusion.2), channel_id=1, source_target_pairs={{0,128},{1,129},{2,130},{3,131},{4,132},{5,133},{6,134},{7,135},{8... | collective-permute-start | bytes 1572872 | tf_op jit(solution)/shard_map/ppermute | solution.py:42
  47.1 2.6 %mix_rows.1 = (f32[512,256]{1,0:T(8,128)S(1)}, f32[128,256]{1,0:T(8,128)S(1)}, f32[128,256]{1,0:T(8,128)S(1)}, f32[512,256]{1,0:T(8,128)S(1)}) custom-call(f32[1280,256]{1,0:T(8,128)S(1)} %pad_maximum_fusion.xf, f32[1280,256]{1,0:T(8,128)} %collective-permute-done.9.xg, f32[512,256]{1,0:T(8,128)S(1)} %copy-done.2, s32[10,128]{1,0:T(8,128)S(1)} %pad_add_fusion.mask, ...), custom_call_target="tpu_custom_call" | custom-call | flops 1 | bytes 1 | tf_op jit(solution)/shard_map/mix_rows/pallas_call | solution.py:142
  49.7 1.9 %collective-permute-start.12 = (f32[512,256]{1,0:T(8,128)S(1)}, f32[512,256]{1,0:T(8,128)S(1)}, u32[]{:S(2)}, u32[]{:S(2)}) collective-permute-start(f32[512,256]{1,0:T(8,128)S(1)} %get-tuple-element.37.rest_3_), channel_id=1, source_target_pairs={{0,2},{2,4},{4,6},{6,8},{8,10},{10,12},{12,14},{14,16},{16,18},{18... | collective-permute-start | bytes 1572872 | tf_op jit(solution)/shard_map/ppermute | solution.py:439
  51.6 5.8 %collective-permute-start.13 = (f32[512,256]{1,0:T(8,128)S(1)}, f32[512,256]{1,0:T(8,128)S(1)}, u32[]{:S(2)}, u32[]{:S(2)}) collective-permute-start(f32[512,256]{1,0:T(8,128)S(1)} %get-tuple-element.34.rest_0_), channel_id=1, source_target_pairs={{2,0},{4,2},{6,4},{8,6},{10,8},{12,10},{14,12},{16,14},{18,16},{20... | collective-permute-start | bytes 1572872 | tf_op jit(solution)/shard_map/ppermute | solution.py:440
  57.4 3.9 %early_tiles.1.total_in = f32[16,128,256]{2,1,0:T(8,128)S(1)} custom-call(s32[1,64]{1,0:T(1,128)S(1)} %copy-done.8, s32[1,64]{1,0:T(1,128)S(1)} %copy-done.9, f32[64,128,128]{2,1,0:T(8,128)S(1)} %bitcast.12, f32[512,256]{1,0:T(8,128)S(1)} %get-tuple-element.34.rest_0_, f32[128,256]{1,0:T(8,128)S(1)} %get-tuple-element.35.rest_1_, ...), custom_call_target="tpu_custom_call" | custom-call | flops 1 | bytes 1 | tf_op jit(solution)/shard_map/early_tiles/pallas_call | solution.py:253
  61.3 14.2 %collective-permute-done.7.rest_1_ = f32[512,256]{1,0:T(8,128)S(1)} collective-permute-done((f32[512,256]{1,0:T(8,128)S(1)}, f32[512,256]{1,0:T(8,128)S(1)}, u32[]{:S(2)}, u32[]{:S(2)}) %collective-permute-start.7) | collective-permute-done | bytes 524320 | tf_op jit(solution)/shard_map/ppermute | solution.py:42
  76.8 5.2 %late_tiles.1.total_in = f32[16,128,256]{2,1,0:T(8,128)S(1)} custom-call(s32[1,64]{1,0:T(1,128)S(1)} %copy-done.8, s32[1,64]{1,0:T(1,128)S(1)} %copy-done.9, f32[64,128,128]{2,1,0:T(8,128)S(1)} %bitcast.13, f32[512,256]{1,0:T(8,128)S(1)} %collective-permute-done.12.prev, f32[512,256]{1,0:T(8,128)S(1)} %collective-permute-done.13.after, ...), custom_call_target="tpu_custom_call" | custom-call | flops 1 | bytes 1 | tf_op jit(solution)/shard_map/late_tiles/pallas_call | solution.py:308
  82.1 7.8 %final_tiles.1 = (f32[2048,256]{1,0:T(8,128)S(1)}, f32[32,128]{1,0:T(8,128)S(1)}) custom-call(s32[1]{0:T(128)S(6)} %copy.20.live_ref, s32[1,64]{1,0:T(1,128)S(1)} %copy-done.12, s32[1,64]{1,0:T(1,128)S(1)} %copy-done.13, f32[64,128,128]{2,1,0:T(8,128)S(1)} %bitcast.14, s32[16,128]{1,0:T(8,128)S(1)} %bitcast.16, f32[1,256]{1,0:T(1,128)S(1)} %bitcast.18, ...), custom_call_target="tpu_custom_call" | custom-call | flops 1 | bytes 1 | tf_op jit(solution)/shard_map/final_tiles/pallas_call | solution.py:390
  91.1 4.3 %collective-permute-done.16.refs_2_ = f32[32,128]{1,0:T(8,128)S(1)} collective-permute-done((f32[32,128]{1,0:T(8,128)S(1)}, f32[32,128]{1,0:T(8,128)S(1)}, u32[]{:S(2)}, u32[]{:S(2)}) %collective-permute-start.16) | collective-permute-done | bytes 16416 | tf_op jit(solution)/shard_map/ppermute | solution.py:42
  95.4 1.9 %normalise.1 = f32[2048,256]{1,0:T(8,128)} custom-call(f32[2048,256]{1,0:T(8,128)S(1)} %get-tuple-element.45.refs_0_, f32[32,128]{1,0:T(8,128)S(1)} %get-tuple-element.46.refs_1_, f32[32,128]{1,0:T(8,128)S(1)} %collective-permute-done.16.refs_2_, f32[1,256]{1,0:T(1,128)S(1)} %bitcast.20), custom_call_target="tpu_custom_call" | custom-call | flops 1 | bytes 1 | tf_op jit(solution)/shard_map/normalise/pallas_call | solution.py:426
  (62 shorter events, 7.8 us)
Async XLA Ops:
  2.8 5.8 %collective-permute-start = (f32[40,256]{1,0:T(8,128)}, f32[40,256]{1,0:T(8,128)S(1)}, u32[]{:S(2)}, u32[]{:S(2)}) collective-permute-start(f32[40,256]{1,0:T(8,128)} %hub_rows.2.own_f), channel_id=1, source_target_pairs={{0,1},{1,0},{2,3},{3,2},{4,5},{5,4},{6,7},{7,6},{8,9},{9,8},{10,11... | collective-permute-start | bytes 122888 | tf_op jit(solution)/shard_map/ppermute | solution.py:42
  5.2 4.2 %collective-permute-start.1 = (f32[40,256]{1,0:T(8,128)}, f32[40,256]{1,0:T(8,128)S(1)}, u32[]{:S(2)}, u32[]{:S(2)}) collective-permute-start(f32[40,256]{1,0:T(8,128)} %hub_rows.2.own_f), channel_id=1, source_target_pairs={{0,32},{1,33},{2,34},{3,35},{4,36},{5,37},{6,38},{7,39},{8,40},{9,... | collective-permute-start | bytes 122888 | tf_op jit(solution)/shard_map/ppermute | solution.py:42
  6.6 4.2 %collective-permute-start.2 = (f32[40,256]{1,0:T(8,128)}, f32[40,256]{1,0:T(8,128)S(1)}, u32[]{:S(2)}, u32[]{:S(2)}) collective-permute-start(f32[40,256]{1,0:T(8,128)} %hub_rows.2.own_f), channel_id=1, source_target_pairs={{0,33},{1,32},{2,35},{3,34},{4,37},{5,36},{6,39},{7,38},{8,41},{9,... | collective-permute-start | bytes 122888 | tf_op jit(solution)/shard_map/ppermute | solution.py:42
  8.1 36.1 %copy-start.5 = (s32[2048]{0:T(1024)S(1)}, s32[2048]{0:T(1024)}, u32[]{:S(2)}) copy-start(s32[2048]{0:T(1024)} %mask.1) | copy-start | bytes 24580
  10.8 30.7 %collective-permute-start.9 = (f32[1280,256]{1,0:T(8,128)S(1)}, f32[1280,256]{1,0:T(8,128)}, u32[]{:S(2)}, u32[]{:S(2)}) collective-permute-start(f32[1280,256]{1,0:T(8,128)S(1)} %pad_maximum_fusion.xf), channel_id=1, source_target_pairs={{0,1},{1,0},{2,3},{3,2},{4,5},{5,4},{6,7},{7,6},{8,9},{9,8},{10,11... | collective-permute-start | bytes 3932168 | tf_op jit(solution)/shard_map/ppermute | solution.py:42
  15.5 27.6 %copy-start.4 = (f32[768,256]{1,0:T(8,128)S(1)}, f32[768,256]{1,0:T(8,128)}, u32[]{:S(2)}) copy-start(f32[768,256]{1,0:T(8,128)} %slice.39.xf) | copy-start | bytes 2359300
  15.5 31.6 %copy-start.2 = (f32[512,256]{1,0:T(8,128)S(1)}, f32[512,256]{1,0:T(8,128)}, u32[]{:S(2)}) copy-start(f32[512,256]{1,0:T(8,128)} %weight.5) | copy-start | bytes 1572868
  15.5 31.6 %copy-start.6 = (f32[8,256]{1,0:T(8,128)S(1)}, f32[8,256]{1,0:T(8,128)}, u32[]{:S(2)}) copy-start(f32[8,256]{1,0:T(8,128)} %get-tuple-element.33.token_y) | copy-start | bytes 24580
  15.5 8.5 %collective-permute-start.3 = (f32[64,256]{1,0:T(8,128)}, f32[64,256]{1,0:T(8,128)S(1)}, u32[]{:S(2)}, u32[]{:S(2)}) collective-permute-start(f32[64,256]{1,0:T(8,128)} %get-tuple-element.29), channel_id=1, source_target_pairs={{0,16},{1,17},{2,18},{3,19},{4,20},{5,21},{6,22},{7,23},{8,24},{9,... | collective-permute-start | bytes 196616 | tf_op jit(solution)/shard_map/ppermute | solution.py:42
  24.0 8.8 %collective-permute-start.4 = (f32[128,256]{1,0:T(8,128)S(1)}, f32[128,256]{1,0:T(8,128)S(1)}, u32[]{:S(2)}, u32[]{:S(2)}) collective-permute-start(f32[128,256]{1,0:T(8,128)S(1)} %get-tuple-element.49), channel_id=1, source_target_pairs={{0,4},{1,5},{2,6},{3,7},{4,8},{5,9},{6,10},{7,11},{8,12},{9,13},{1... | collective-permute-start | bytes 393224 | tf_op jit(solution)/shard_map/ppermute | solution.py:42
  25.0 7.8 %collective-permute-start.5 = (f32[128,256]{1,0:T(8,128)S(1)}, f32[128,256]{1,0:T(8,128)S(1)}, u32[]{:S(2)}, u32[]{:S(2)}) collective-permute-start(f32[128,256]{1,0:T(8,128)S(1)} %get-tuple-element.49), channel_id=1, source_target_pairs={{0,28},{1,29},{2,30},{3,31},{4,0},{5,1},{6,2},{7,3},{8,4},{9,5},{1... | collective-permute-start | bytes 393224 | tf_op jit(solution)/shard_map/ppermute | solution.py:42
  28.6 8.0 %collective-permute-start.6 = (f32[128,256]{1,0:T(8,128)S(1)}, f32[128,256]{1,0:T(8,128)S(1)}, u32[]{:S(2)}, u32[]{:S(2)}) collective-permute-start(f32[128,256]{1,0:T(8,128)S(1)} %get-tuple-element.49), channel_id=1, source_target_pairs={{0,8},{1,9},{2,10},{3,11},{4,12},{5,13},{6,14},{7,15},{8,16},{9,17... | collective-permute-start | bytes 393224 | tf_op jit(solution)/shard_map/ppermute | solution.py:42
  36.5 2.0 %collective-permute-start.8 = (f32[512,256]{1,0:T(8,128)S(1)}, f32[512,256]{1,0:T(8,128)S(1)}, u32[]{:S(2)}, u32[]{:S(2)}) collective-permute-start(f32[512,256]{1,0:T(8,128)S(1)} %constant_dynamic-update-slice_fusion.2), channel_id=1, source_target_pairs={{0,2},{1,3},{2,0},{3,1},{4,6},{5,7},{6,4},{7,5},{8,10},{9,11},{10,... | collective-permute-start | bytes 1572872 | tf_op jit(solution)/shard_map/ppermute | solution.py:42
  41.5 15.9 %copy-start.1 = (f32[1,64,128,128]{3,2,1,0:T(8,128)S(1)}, f32[1,64,128,128]{3,2,1,0:T(8,128)}, u32[]{:S(2)}) copy-start(f32[1,64,128,128]{3,2,1,0:T(8,128)} %param.19) | copy-start | bytes 12582916
  41.6 15.8 %copy-start.8 = (s32[1,64]{1,0:T(1,128)S(1)}, s32[1,64]{1,0:T(1,128)}, u32[]{:S(2)}) copy-start(s32[1,64]{1,0:T(1,128)} %rows.3) | copy-start | bytes 772
  41.6 15.8 %copy-start.9 = (s32[1,64]{1,0:T(1,128)S(1)}, s32[1,64]{1,0:T(1,128)}, u32[]{:S(2)}) copy-start(s32[1,64]{1,0:T(1,128)} %cols.3) | copy-start | bytes 772
  41.6 33.9 %collective-permute-start.10 = (f32[2,512,256]{2,1,0:T(8,128)S(1)}, f32[2,512,256]{2,1,0:T(8,128)S(1)}, u32[]{:S(2)}, u32[]{:S(2)}) collective-permute-start(f32[2,512,256]{2,1,0:T(8,128)S(1)} %pad_maximum_fusion.1.rest_0_), channel_id=1, source_target_pairs={{0,64},{1,65},{2,194},{3,195},{4,68},{5,69},{6,198},{7,199},{8,72}... | collective-permute-start | bytes 3145736 | tf_op jit(solution)/shard_map/ppermute | solution.py:42
  43.1 32.4 %collective-permute-start.11 = (f32[768,256]{1,0:T(8,128)S(1)}, f32[768,256]{1,0:T(8,128)S(1)}, u32[]{:S(2)}, u32[]{:S(2)}) collective-permute-start(f32[768,256]{1,0:T(8,128)S(1)} %copy-done.4), channel_id=1, source_target_pairs={{0,1},{1,0},{2,3},{3,2},{4,5},{5,4},{6,7},{7,6},{8,9},{9,8},{10,11... | collective-permute-start | bytes 2359304 | tf_op jit(solution)/shard_map/ppermute | solution.py:42
  44.3 31.2 %collective-permute-start.7 = (f32[512,256]{1,0:T(8,128)S(1)}, f32[512,256]{1,0:T(8,128)S(1)}, u32[]{:S(2)}, u32[]{:S(2)}) collective-permute-start(f32[512,256]{1,0:T(8,128)S(1)} %constant_dynamic-update-slice_fusion.2), channel_id=1, source_target_pairs={{0,128},{1,129},{2,130},{3,131},{4,132},{5,133},{6,134},{7,135},{8... | collective-permute-start | bytes 1572872 | tf_op jit(solution)/shard_map/ppermute | solution.py:42
  49.7 25.8 %collective-permute-start.12 = (f32[512,256]{1,0:T(8,128)S(1)}, f32[512,256]{1,0:T(8,128)S(1)}, u32[]{:S(2)}, u32[]{:S(2)}) collective-permute-start(f32[512,256]{1,0:T(8,128)S(1)} %get-tuple-element.37.rest_3_), channel_id=1, source_target_pairs={{0,2},{2,4},{4,6},{6,8},{8,10},{10,12},{12,14},{14,16},{16,18},{18... | collective-permute-start | bytes 1572872 | tf_op jit(solution)/shard_map/ppermute | solution.py:439
  51.6 23.9 %collective-permute-start.13 = (f32[512,256]{1,0:T(8,128)S(1)}, f32[512,256]{1,0:T(8,128)S(1)}, u32[]{:S(2)}, u32[]{:S(2)}) collective-permute-start(f32[512,256]{1,0:T(8,128)S(1)} %get-tuple-element.34.rest_0_), channel_id=1, source_target_pairs={{2,0},{4,2},{6,4},{8,6},{10,8},{12,10},{14,12},{16,14},{18,16},{20... | collective-permute-start | bytes 1572872 | tf_op jit(solution)/shard_map/ppermute | solution.py:440
  75.5 6.5 %collective-permute-start.15 = (f32[2,512,256]{2,1,0:T(8,128)S(1)}, f32[2,512,256]{2,1,0:T(8,128)S(1)}, u32[]{:S(2)}, u32[]{:S(2)}) collective-permute-start(f32[2,512,256]{2,1,0:T(8,128)S(1)} %collective-permute-done.10.rest_3_), channel_id=1, source_target_pairs={{0,2},{1,3},{2,0},{3,1},{4,6},{5,7},{6,4},{7,5},{8,10},{9,11},{10,... | collective-permute-start | bytes 3145736 | tf_op jit(solution)/shard_map/ppermute | solution.py:42
  75.6 6.4 %collective-permute-start.14 = (f32[512,256]{1,0:T(8,128)S(1)}, f32[512,256]{1,0:T(8,128)S(1)}, u32[]{:S(2)}, u32[]{:S(2)}) collective-permute-start(f32[512,256]{1,0:T(8,128)S(1)} %collective-permute-done.7.rest_1_), channel_id=1, source_target_pairs={{0,2},{1,3},{2,0},{3,1},{4,6},{5,7},{6,4},{7,5},{8,10},{9,11},{10,... | collective-permute-start | bytes 1572872 | tf_op jit(solution)/shard_map/ppermute | solution.py:42
  90.0 5.5 %collective-permute-start.16 = (f32[32,128]{1,0:T(8,128)S(1)}, f32[32,128]{1,0:T(8,128)S(1)}, u32[]{:S(2)}, u32[]{:S(2)}) collective-permute-start(f32[32,128]{1,0:T(8,128)S(1)} %get-tuple-element.46.refs_1_), channel_id=1, source_target_pairs={{0,1},{1,0},{2,3},{3,2},{4,5},{5,4},{6,7},{7,6},{8,9},{9,8},{10,11... | collective-permute-start | bytes 49160 | tf_op jit(solution)/shard_map/ppermute | solution.py:42
  (10 other events, 58.3 us)

commit v3 on v2

--- a/solution.py
+++ b/solution.py
@@ -201,17 +201,17 @@
     lax.fori_loop(0, (count + UNROLL - 1) // UNROLL, step, 0)
 
 
-def list_tiles(cols, wanted, listed):
+def list_tiles(wanted, listed):
     def clear(t, carry):
         listed[t] = 0
         return carry
 
     def step(t, n):
         listed[n] = t
-        return n + jnp.where(wanted(cols[0, t]), 1, 0)
+        return n + jnp.where(wanted(t), 1, 0)
 
     lax.fori_loop(0, listed.shape[0], clear, 0)
-    return lax.fori_loop(0, cols.shape[1], step, 0)
+    return lax.fori_loop(0, listed.shape[0] - UNROLL, step, 0)
 
 
 def inside(col, low, high):
@@ -232,7 +232,8 @@
     blocks = total.shape[0]
     fill_blocks(ext, 0, parts)
 
-    def wanted(col):
+    def wanted(t):
+        col = cols[0, t]
         return jnp.logical_or(inside(col, blocks, low), inside(col, high, 2 * blocks))
 
     def y_of(t):
@@ -240,7 +241,7 @@
         at = col - blocks - jnp.where(col >= high, high - low, 0)
         return ext[jnp.clip(at, 0, ext.shape[0] - 1)]
 
-    count = list_tiles(cols, wanted, listed)
+    count = list_tiles(wanted, listed)
     gathered_sum(
         count, lambda k: listed[k], lambda t: rows[0, t], lambda t: tiles[t], y_of, total
     )
@@ -266,22 +267,17 @@
 
 
 def late_kernel(
-    late, rows, cols, tiles, prev, after, xf, xg, weight, mask, token_y, total_in, total, ext, listed
+    late, rows, cols, tiles, prev, after, y_mid, total_in, total, ext, listed
 ):
     total[...] = total_in[...]
     low, high = late
-    marks = mask[...].astype(F32)
     blocks = total.shape[0]
     size = high - low
     reach = prev.shape[0] // 128
-    fill_blocks(ext, size, (prev, after))
-
-    def store(b, y):
-        ext[b] = y
-
-    mix_into(xf, xg, weight, marks[low - blocks : high - blocks], token_y, store)
-
-    def wanted(col):
+    fill_blocks(ext, 0, (y_mid, prev, after))
+
+    def wanted(t):
+        col = cols[0, t]
         return jnp.logical_or(
             inside(col, low, high), jnp.logical_or(col < blocks, col >= 2 * blocks)
         )
@@ -295,20 +291,20 @@
         )
         return ext[jnp.clip(at, 0, ext.shape[0] - 1)]
 
-    count = list_tiles(cols, wanted, listed)
+    count = list_tiles(wanted, listed)
     gathered_sum(
         count, lambda k: listed[k], lambda t: rows[0, t], lambda t: tiles[t], y_of, total
     )
 
 
-def late_sum(late, rows, cols, tiles, prev, after, xf, xg, weight, mask, token_y, total):
-    half = xf.shape[1]
+def late_sum(late, rows, cols, tiles, prev, after, y_mid, total):
+    half = y_mid.shape[1]
     count = tiles.shape[0]
     depth = late[1] - late[0] + (prev.shape[0] + after.shape[0]) // 128
     return pl.pallas_call(
         functools.partial(late_kernel, late),
         out_shape=jax.ShapeDtypeStruct(total.shape, F32),
-        in_specs=[SMEM, SMEM] + [VMEM] * 9,
+        in_specs=[SMEM, SMEM] + [VMEM] * 5,
         out_specs=VMEM,
         scratch_shapes=[
             pltpu.VMEM((depth, 128, half), F32),
@@ -317,9 +313,10 @@
         name="late_tiles",
         cost_estimate=LIGHT,
         compiler_params=pltpu.CompilerParams(vmem_limit_bytes=24 << 20),
-    )(rows, cols, tiles, prev, after, xf, xg, weight, mask, token_y, total)
-
-
+    )(rows, cols, tiles, prev, after, y_mid, total)
+
+
+UNIT_OF_KIND = 0b01111000
 PART_AT = (0, 2, 3, 4, 6)
 
 
@@ -343,23 +340,22 @@
 
     def panel(t):
         p = panels[0, t]
-        px = p // 8
-        pyl = (p // 4) % 2
-        kx = (px - x + NX) % NX
+        kx = ((p >> 3) - x) & 3
+        holder = (kx >> 1) ^ 1
+        odd = (kx & 1) == 1
+        slots = [
+            jnp.where(odd, 4 + 2 * (holder ^ c) + (holder ^ pc), kx + (pc ^ c)) for pc in range(2)
+        ]
         slabs = []
-        for k in range(4):
-            pz = 2 * (p % 4) + k // 2
-            pc = k % 2
-            kind = (pz - z + NZ) % 4
-            offset = jnp.where(kind < 2, kind, kind - 4)
-            far = ((pz - z - offset + 2 * NZ) % NZ) // 4
-            unit = jnp.where(kind == 0, 0, jnp.where(kind == 3, 1, kind + 1))
-            unit = jnp.where(kind == 2, 3, unit)
-            holder = jnp.where(kx == 3, 0, 1)
-            other = 4 + jnp.where(holder == c, 0, 2) + jnp.where(holder == pc, 0, 1)
-            slot = jnp.where(kx % 2 == 1, other, kx + (pc + c) % 2)
-            row = unit * 128 + far * 64 + pyl * hubs
-            slabs.append(held[slot, pl.ds(pl.multiple_of(row, hubs), hubs), :])
+        for dz in range(2):
+            delta = 2 * (p & 3) + dz - z
+            kind = delta & 3
+            offset = ((kind + 2) & 3) - 2
+            far = ((delta - offset) >> 2) & 1
+            unit = (UNIT_OF_KIND >> (2 * kind)) & 3
+            row = unit * 128 + far * 64 + ((p >> 2) & 1) * hubs
+            for pc in range(2):
+                slabs.append(held[slots[pc], pl.ds(pl.multiple_of(row, hubs), hubs), :])
         return jnp.concatenate(slabs, 0)
 
     gathered_sum(
@@ -495,7 +491,6 @@
     y_first, y_left, y_right, y_last = mix(
         chunks[0], chunks_g[0], mix_weight, marks, token_y, (edge, inner, inner, edge)
     )
-    prev, after = neighbours(y_first, y_last)
     late = (blocks + wide // 128, 2 * blocks - wide // 128)
     total = early_sum(
         late,
@@ -505,23 +500,20 @@
         (y_first, y_left, y_right, y_last),
         blocks,
     )
-    across, beside, total, chunks_g[1], prev, after = lax.optimization_barrier(
-        (across, beside, total, chunks_g[1], prev, after)
-    )
-    parts = (pair, across, sibling(across), beside, sibling(beside))
-    total = late_sum(
-        late,
-        local_rows,
-        local_cols,
-        local_tiles[0],
-        prev,
-        after,
+    across, y_first, y_last, total = lax.optimization_barrier((across, y_first, y_last, total))
+    prev, after = neighbours(y_first, y_last)
+    (y_mid,) = mix(
         chunks[1],
         chunks_g[1],
         mix_weight,
-        mask,
+        mask[wide // 128 : blocks - wide // 128],
         token_y,
-        total,
+        (rows - 2 * wide,),
+    )
+    beside, y_mid, prev, after = lax.optimization_barrier((beside, y_mid, prev, after))
+    parts = (pair, across, sibling(across), beside, sibling(beside))
+    total = late_sum(
+        late, local_rows, local_cols, local_tiles[0], prev, after, y_mid, total
     )
     hidden, stats = final(
         (hub_count, hub_rows, hub_panels),

time: 97 us -> 90.3 us (0.931)
  the two profiles are of different devices: /device:TPU:8 before, /device:TPU:1 now
where the time goes in v3:
time: 90.3 us; the launch traced here: 89.2 us
  starting transfers between devices  36.5 us (40%)
  Pallas kernels  25.1 us (28%)
  waiting for transfers between devices  23.8 us (26%)
  local copies, waits for them, and re-layouts  2.58 us (3%)
  between operations  0.98 us (1%)
    ppermute x15, starting transfers between devices, send(): return lax.ppermute(value, BOTH, shift(move))  32.1 us
    ppermute x15, waiting for transfers between devices, send(): return lax.ppermute(value, BOTH, shift(move))  23.8 us
    pallas_call x1, Pallas kernels, final(): pl.pallas_call(final_kernel, out_shape=[jax.ShapeDtypeStruct((n, half), F...  6.49 us
    pallas_call x1, Pallas kernels, early_sum(): pl.pallas_call(functools.partial(early_kernel, late), out_shape=jax.Shape...  4.46 us
    pallas_call x1, Pallas kernels, late_sum(): pl.pallas_call(functools.partial(late_kernel, late), out_shape=jax.ShapeD...  3.97 us
    pallas_call x2, Pallas kernels, mix(): pl.pallas_call(mix_kernel, out_shape=[jax.ShapeDtypeStruct((size, half),...  3.39 us
    pallas_call x1, Pallas kernels, hub_rows_of(): pl.pallas_call(hub_rows_kernel, out_shape=jax.ShapeDtypeStruct((count + 8...  2.81 us
    ppermute x1, starting transfers between devices, neighbours(): prev = lax.ppermute(last, 'dom', [(i, i + 1) for i in range(doms - 1)])  2.48 us
  transfers between devices with their start and end apart: 17, of which 8 were waited for; matrix products, arithmetic and copies ran while one was open for 2% of the time, Pallas kernels for 16%

profile of v3, /device:TPU:1, one launch (start us, length us, event | category | flops | bytes accessed | tf_op | source)
XLA Modules:
  0.0 89.2 jit_solution(809593714157640055)
XLA Ops:
  0.0 2.8 %hub_rows.2.own_f = f32[40,256]{1,0:T(8,128)} custom-call(s32[32]{0:T(128)} %ids.1, s32[2048]{0:T(1024)} %mask.1, f32[2048,256]{1,0:T(8,128)} %features.3, f32[1,256]{1,0:T(1,128)} %bitcast.18), custom_call_target="tpu_custom_call" | custom-call | flops 1 | bytes 1 | tf_op jit(solution)/shard_map/hub_rows/pallas_call | solution.py:85
  2.8 3.8 %collective-permute-start = (f32[40,256]{1,0:T(8,128)}, f32[40,256]{1,0:T(8,128)S(1)}, u32[]{:S(2)}, u32[]{:S(2)}) collective-permute-start(f32[40,256]{1,0:T(8,128)} %hub_rows.2.own_f), channel_id=1, source_target_pairs={{0,1},{1,0},{2,3},{3,2},{4,5},{5,4},{6,7},{7,6},{8,9},{9,8},{10,11... | collective-permute-start | bytes 122888 | tf_op jit(solution)/shard_map/ppermute | solution.py:42
  8.6 1.5 %collective-permute-done.1.other_f = f32[40,256]{1,0:T(8,128)S(1)} collective-permute-done((f32[40,256]{1,0:T(8,128)}, f32[40,256]{1,0:T(8,128)S(1)}, u32[]{:S(2)}, u32[]{:S(2)}) %collective-permute-start.1) | collective-permute-done | bytes 40992 | tf_op jit(solution)/shard_map/ppermute | solution.py:42
  10.1 1.5 %collective-permute-done.2.other_g = f32[40,256]{1,0:T(8,128)S(1)} collective-permute-done((f32[40,256]{1,0:T(8,128)}, f32[40,256]{1,0:T(8,128)S(1)}, u32[]{:S(2)}, u32[]{:S(2)}) %collective-permute-start.2) | collective-permute-done | bytes 40992 | tf_op jit(solution)/shard_map/ppermute | solution.py:42
  12.2 2.1 %mix_hub.1 = (f32[64,256]{1,0:T(8,128)}, f32[8,256]{1,0:T(8,128)}) custom-call(f32[40,256]{1,0:T(8,128)} %hub_rows.2.own_f, f32[40,256]{1,0:T(8,128)} %copy-done.14, f32[40,256]{1,0:T(8,128)} %copy-done.15, f32[40,256]{1,0:T(8,128)} %copy-done.16, f32[512,256]{1,0:T(8,128)} %weight.5), custom_call_target="tpu_custom_call" | custom-call | flops 1 | bytes 1 | tf_op jit(solution)/shard_map/mix_hub/pallas_call | solution.py:166
  14.3 6.7 %collective-permute-start.3 = (f32[64,256]{1,0:T(8,128)}, f32[64,256]{1,0:T(8,128)S(1)}, u32[]{:S(2)}, u32[]{:S(2)}) collective-permute-start(f32[64,256]{1,0:T(8,128)} %get-tuple-element.31), channel_id=1, source_target_pairs={{0,16},{1,17},{2,18},{3,19},{4,20},{5,21},{6,22},{7,23},{8,24},{9,... | collective-permute-start | bytes 196616 | tf_op jit(solution)/shard_map/ppermute | solution.py:42
  23.7 3.4 %collective-permute-start.5 = (f32[128,256]{1,0:T(8,128)S(1)}, f32[128,256]{1,0:T(8,128)S(1)}, u32[]{:S(2)}, u32[]{:S(2)}) collective-permute-start(f32[128,256]{1,0:T(8,128)S(1)} %get-tuple-element.53), channel_id=1, source_target_pairs={{0,28},{1,29},{2,30},{3,31},{4,0},{5,1},{6,2},{7,3},{8,4},{9,5},{1... | collective-permute-start | bytes 393224 | tf_op jit(solution)/shard_map/ppermute | solution.py:42
  27.1 2.7 %collective-permute-done.4 = f32[128,256]{1,0:T(8,128)S(1)} collective-permute-done((f32[128,256]{1,0:T(8,128)S(1)}, f32[128,256]{1,0:T(8,128)S(1)}, u32[]{:S(2)}, u32[]{:S(2)}) %collective-permute-start.4) | collective-permute-done | bytes 131104 | tf_op jit(solution)/shard_map/ppermute | solution.py:42
  29.8 4.9 %collective-permute-done.6 = f32[128,256]{1,0:T(8,128)S(1)} collective-permute-done((f32[128,256]{1,0:T(8,128)S(1)}, f32[128,256]{1,0:T(8,128)S(1)}, u32[]{:S(2)}, u32[]{:S(2)}) %collective-permute-start.6) | collective-permute-done | bytes 131104 | tf_op jit(solution)/shard_map/ppermute | solution.py:42
  34.7 4.5 %collective-permute-start.7 = (f32[512,256]{1,0:T(8,128)S(1)}, f32[512,256]{1,0:T(8,128)S(1)}, u32[]{:S(2)}, u32[]{:S(2)}) collective-permute-start(f32[512,256]{1,0:T(8,128)S(1)} %constant_dynamic-update-slice_fusion.2), channel_id=1, source_target_pairs={{0,2},{1,3},{2,0},{3,1},{4,6},{5,7},{6,4},{7,5},{8,10},{9,11},{10,... | collective-permute-start | bytes 1572872 | tf_op jit(solution)/shard_map/ppermute | solution.py:42
  39.3 2.8 %collective-permute-start.11 = (f32[512,256]{1,0:T(8,128)S(1)}, f32[512,256]{1,0:T(8,128)S(1)}, u32[]{:S(2)}, u32[]{:S(2)}) collective-permute-start(f32[512,256]{1,0:T(8,128)S(1)} %constant_dynamic-update-slice_fusion.2), channel_id=1, source_target_pairs={{0,128},{1,129},{2,130},{3,131},{4,132},{5,133},{6,134},{7,135},{8... | collective-permute-start | bytes 1572872 | tf_op jit(solution)/shard_map/ppermute | solution.py:42
  42.1 1.4 %collective-permute-start.9 = (f32[2,512,256]{2,1,0:T(8,128)S(1)}, f32[2,512,256]{2,1,0:T(8,128)S(1)}, u32[]{:S(2)}, u32[]{:S(2)}) collective-permute-start(f32[2,512,256]{2,1,0:T(8,128)S(1)} %pad_maximum_fusion.1.rest_0_), channel_id=1, source_target_pairs={{0,64},{1,65},{2,194},{3,195},{4,68},{5,69},{6,198},{7,199},{8,72}... | collective-permute-start | bytes 3145736 | tf_op jit(solution)/shard_map/ppermute | solution.py:42
  43.5 2.6 %collective-permute-start.10 = (f32[768,256]{1,0:T(8,128)S(1)}, f32[768,256]{1,0:T(8,128)S(1)}, u32[]{:S(2)}, u32[]{:S(2)}) collective-permute-start(f32[768,256]{1,0:T(8,128)S(1)} %copy-done.4), channel_id=1, source_target_pairs={{0,1},{1,0},{2,3},{3,2},{4,5},{5,4},{6,7},{7,6},{8,9},{9,8},{10,11... | collective-permute-start | bytes 2359304 | tf_op jit(solution)/shard_map/ppermute | solution.py:42
  46.1 2.6 %mix_rows.3 = (f32[512,256]{1,0:T(8,128)S(1)}, f32[128,256]{1,0:T(8,128)S(1)}, f32[128,256]{1,0:T(8,128)S(1)}, f32[512,256]{1,0:T(8,128)S(1)}) custom-call(f32[1280,256]{1,0:T(8,128)S(1)} %pad_maximum_fusion.xf, f32[1280,256]{1,0:T(8,128)} %collective-permute-done.8.xg, f32[512,256]{1,0:T(8,128)S(1)} %copy-done.2, s32[10,128]{1,0:T(8,128)S(1)} %pad_add_fusion.mask, ...), custom_call_target="tpu_custom_call" | custom-call | flops 1 | bytes 1 | tf_op jit(solution)/shard_map/mix_rows/pallas_call | solution.py:142
  48.7 4.5 %early_tiles.1.total_in = f32[16,128,256]{2,1,0:T(8,128)S(1)} custom-call(s32[1,64]{1,0:T(1,128)S(1)} %copy-done.8, s32[1,64]{1,0:T(1,128)S(1)} %copy-done.9, f32[64,128,128]{2,1,0:T(8,128)S(1)} %bitcast.14, f32[512,256]{1,0:T(8,128)S(1)} %get-tuple-element.42.rest_0_, f32[128,256]{1,0:T(8,128)S(1)} %get-tuple-element.39.rest_1_, ...), custom_call_target="tpu_custom_call" | custom-call | flops 1 | bytes 1 | tf_op jit(solution)/shard_map/early_tiles/pallas_call | solution.py:254
  54.3 2.5 %collective-permute-start.12 = (f32[512,256]{1,0:T(8,128)S(1)}, f32[512,256]{1,0:T(8,128)S(1)}, u32[]{:S(2)}, u32[]{:S(2)}) collective-permute-start(f32[512,256]{1,0:T(8,128)S(1)} %get-tuple-element.41.rest_3_), channel_id=1, source_target_pairs={{0,2},{2,4},{4,6},{6,8},{8,10},{10,12},{12,14},{14,16},{16,18},{18... | collective-permute-start | bytes 1572872 | tf_op jit(solution)/shard_map/ppermute | solution.py:435
  56.8 1.9 %collective-permute-start.13 = (f32[512,256]{1,0:T(8,128)S(1)}, f32[512,256]{1,0:T(8,128)S(1)}, u32[]{:S(2)}, u32[]{:S(2)}) collective-permute-start(f32[512,256]{1,0:T(8,128)S(1)} %get-tuple-element.42.rest_0_), channel_id=1, source_target_pairs={{2,0},{4,2},{6,4},{8,6},{10,8},{12,10},{14,12},{16,14},{18,16},{20... | collective-permute-start | bytes 1572872 | tf_op jit(solution)/shard_map/ppermute | solution.py:436
  58.7 9.6 %collective-permute-done.10.xg = f32[768,256]{1,0:T(8,128)S(1)} collective-permute-done((f32[768,256]{1,0:T(8,128)S(1)}, f32[768,256]{1,0:T(8,128)S(1)}, u32[]{:S(2)}, u32[]{:S(2)}) %collective-permute-start.10) | collective-permute-done | bytes 786464 | tf_op jit(solution)/shard_map/ppermute | solution.py:42
  69.1 2.4 %collective-permute-start.15 = (f32[2,512,256]{2,1,0:T(8,128)S(1)}, f32[2,512,256]{2,1,0:T(8,128)S(1)}, u32[]{:S(2)}, u32[]{:S(2)}) collective-permute-start(f32[2,512,256]{2,1,0:T(8,128)S(1)} %collective-permute-done.9.rest_3_), channel_id=1, source_target_pairs={{0,2},{1,3},{2,0},{3,1},{4,6},{5,7},{6,4},{7,5},{8,10},{9,11},{10,... | collective-permute-start | bytes 3145736 | tf_op jit(solution)/shard_map/ppermute | solution.py:42
  72.5 4.0 %late_tiles.1.total_in = f32[16,128,256]{2,1,0:T(8,128)S(1)} custom-call(s32[1,64]{1,0:T(1,128)S(1)} %copy-done.8, s32[1,64]{1,0:T(1,128)S(1)} %copy-done.9, f32[64,128,128]{2,1,0:T(8,128)S(1)} %bitcast.15, f32[512,256]{1,0:T(8,128)S(1)} %collective-permute-done.12.prev, f32[512,256]{1,0:T(8,128)S(1)} %collective-permute-done.13.after, ...), custom_call_target="tpu_custom_call" | custom-call | flops 1 | bytes 1 | tf_op jit(solution)/shard_map/late_tiles/pallas_call | solution.py:304
  76.6 6.5 %final_tiles.1 = (f32[2048,256]{1,0:T(8,128)S(1)}, f32[32,128]{1,0:T(8,128)S(1)}) custom-call(s32[1]{0:T(128)S(6)} %copy.20.live_ref, s32[1,64]{1,0:T(1,128)S(1)} %copy-done.12, s32[1,64]{1,0:T(1,128)S(1)} %copy-done.13, f32[64,128,128]{2,1,0:T(8,128)S(1)} %bitcast.16, s32[16,128]{1,0:T(8,128)S(1)} %bitcast.17, f32[1,256]{1,0:T(1,128)S(1)} %bitcast.19, ...), custom_call_target="tpu_custom_call" | custom-call | flops 1 | bytes 1 | tf_op jit(solution)/shard_map/final_tiles/pallas_call | solution.py:386
  83.1 2.7 %collective-permute-start.16 = (f32[32,128]{1,0:T(8,128)S(1)}, f32[32,128]{1,0:T(8,128)S(1)}, u32[]{:S(2)}, u32[]{:S(2)}) collective-permute-start(f32[32,128]{1,0:T(8,128)S(1)} %get-tuple-element.50.refs_1_), channel_id=1, source_target_pairs={{0,1},{1,0},{2,3},{3,2},{4,5},{5,4},{6,7},{7,6},{8,9},{9,8},{10,11... | collective-permute-start | bytes 49160 | tf_op jit(solution)/shard_map/ppermute | solution.py:42
  85.7 1.5 %collective-permute-done.16.refs_2_ = f32[32,128]{1,0:T(8,128)S(1)} collective-permute-done((f32[32,128]{1,0:T(8,128)S(1)}, f32[32,128]{1,0:T(8,128)S(1)}, u32[]{:S(2)}, u32[]{:S(2)}) %collective-permute-start.16) | collective-permute-done | bytes 16416 | tf_op jit(solution)/shard_map/ppermute | solution.py:42
  87.2 1.9 %normalise.1 = f32[2048,256]{1,0:T(8,128)} custom-call(f32[2048,256]{1,0:T(8,128)S(1)} %get-tuple-element.49.refs_0_, f32[32,128]{1,0:T(8,128)S(1)} %get-tuple-element.50.refs_1_, f32[32,128]{1,0:T(8,128)S(1)} %collective-permute-done.16.refs_2_, f32[1,256]{1,0:T(1,128)S(1)} %bitcast.21), custom_call_target="tpu_custom_call" | custom-call | flops 1 | bytes 1 | tf_op jit(solution)/shard_map/normalise/pallas_call | solution.py:422
  (64 shorter events, 7.6 us)
Async XLA Ops:
  0.0 7.4 %copy-start = (f32[2048,256]{1,0:T(8,128)S(1)}, f32[2048,256]{1,0:T(8,128)}, u32[]{:S(2)}) copy-start(f32[2048,256]{1,0:T(8,128)} %features.3) | copy-start | bytes 6291460
  2.8 5.7 %collective-permute-start = (f32[40,256]{1,0:T(8,128)}, f32[40,256]{1,0:T(8,128)S(1)}, u32[]{:S(2)}, u32[]{:S(2)}) collective-permute-start(f32[40,256]{1,0:T(8,128)} %hub_rows.2.own_f), channel_id=1, source_target_pairs={{0,1},{1,0},{2,3},{3,2},{4,5},{5,4},{6,7},{7,6},{8,9},{9,8},{10,11... | collective-permute-start | bytes 122888 | tf_op jit(solution)/shard_map/ppermute | solution.py:42
  6.7 3.4 %collective-permute-start.1 = (f32[40,256]{1,0:T(8,128)}, f32[40,256]{1,0:T(8,128)S(1)}, u32[]{:S(2)}, u32[]{:S(2)}) collective-permute-start(f32[40,256]{1,0:T(8,128)} %hub_rows.2.own_f), channel_id=1, source_target_pairs={{0,32},{1,33},{2,34},{3,35},{4,36},{5,37},{6,38},{7,39},{8,40},{9,... | collective-permute-start | bytes 122888 | tf_op jit(solution)/shard_map/ppermute | solution.py:42
  7.0 4.6 %collective-permute-start.2 = (f32[40,256]{1,0:T(8,128)}, f32[40,256]{1,0:T(8,128)S(1)}, u32[]{:S(2)}, u32[]{:S(2)}) collective-permute-start(f32[40,256]{1,0:T(8,128)} %hub_rows.2.own_f), channel_id=1, source_target_pairs={{0,33},{1,32},{2,35},{3,34},{4,37},{5,36},{6,39},{7,38},{8,41},{9,... | collective-permute-start | bytes 122888 | tf_op jit(solution)/shard_map/ppermute | solution.py:42
  8.5 37.5 %copy-start.5 = (s32[2048]{0:T(1024)S(1)}, s32[2048]{0:T(1024)}, u32[]{:S(2)}) copy-start(s32[2048]{0:T(1024)} %mask.1) | copy-start | bytes 24580
  11.6 30.4 %collective-permute-start.8 = (f32[1280,256]{1,0:T(8,128)S(1)}, f32[1280,256]{1,0:T(8,128)}, u32[]{:S(2)}, u32[]{:S(2)}) collective-permute-start(f32[1280,256]{1,0:T(8,128)S(1)} %pad_maximum_fusion.xf), channel_id=1, source_target_pairs={{0,1},{1,0},{2,3},{3,2},{4,5},{5,4},{6,7},{7,6},{8,9},{9,8},{10,11... | collective-permute-start | bytes 3932168 | tf_op jit(solution)/shard_map/ppermute | solution.py:42
  14.3 29.2 %copy-start.4 = (f32[768,256]{1,0:T(8,128)S(1)}, f32[768,256]{1,0:T(8,128)}, u32[]{:S(2)}) copy-start(f32[768,256]{1,0:T(8,128)} %slice.53.xf) | copy-start | bytes 2359300
  14.3 31.8 %copy-start.2 = (f32[512,256]{1,0:T(8,128)S(1)}, f32[512,256]{1,0:T(8,128)}, u32[]{:S(2)}) copy-start(f32[512,256]{1,0:T(8,128)} %weight.5) | copy-start | bytes 1572868
  14.3 31.8 %copy-start.6 = (f32[8,256]{1,0:T(8,128)S(1)}, f32[8,256]{1,0:T(8,128)}, u32[]{:S(2)}) copy-start(f32[8,256]{1,0:T(8,128)} %get-tuple-element.35.token_y) | copy-start | bytes 24580
  14.3 8.7 %collective-permute-start.3 = (f32[64,256]{1,0:T(8,128)}, f32[64,256]{1,0:T(8,128)S(1)}, u32[]{:S(2)}, u32[]{:S(2)}) collective-permute-start(f32[64,256]{1,0:T(8,128)} %get-tuple-element.31), channel_id=1, source_target_pairs={{0,16},{1,17},{2,18},{3,19},{4,20},{5,21},{6,22},{7,23},{8,24},{9,... | collective-permute-start | bytes 196616 | tf_op jit(solution)/shard_map/ppermute | solution.py:42
  23.0 6.8 %collective-permute-start.4 = (f32[128,256]{1,0:T(8,128)S(1)}, f32[128,256]{1,0:T(8,128)S(1)}, u32[]{:S(2)}, u32[]{:S(2)}) collective-permute-start(f32[128,256]{1,0:T(8,128)S(1)} %get-tuple-element.53), channel_id=1, source_target_pairs={{0,4},{1,5},{2,6},{3,7},{4,8},{5,9},{6,10},{7,11},{8,12},{9,13},{1... | collective-permute-start | bytes 393224 | tf_op jit(solution)/shard_map/ppermute | solution.py:42
  23.7 6.1 %collective-permute-start.5 = (f32[128,256]{1,0:T(8,128)S(1)}, f32[128,256]{1,0:T(8,128)S(1)}, u32[]{:S(2)}, u32[]{:S(2)}) collective-permute-start(f32[128,256]{1,0:T(8,128)S(1)} %get-tuple-element.53), channel_id=1, source_target_pairs={{0,28},{1,29},{2,30},{3,31},{4,0},{5,1},{6,2},{7,3},{8,4},{9,5},{1... | collective-permute-start | bytes 393224 | tf_op jit(solution)/shard_map/ppermute | solution.py:42
  27.1 7.6 %collective-permute-start.6 = (f32[128,256]{1,0:T(8,128)S(1)}, f32[128,256]{1,0:T(8,128)S(1)}, u32[]{:S(2)}, u32[]{:S(2)}) collective-permute-start(f32[128,256]{1,0:T(8,128)S(1)} %get-tuple-element.53), channel_id=1, source_target_pairs={{0,8},{1,9},{2,10},{3,11},{4,12},{5,13},{6,14},{7,15},{8,16},{9,17... | collective-permute-start | bytes 393224 | tf_op jit(solution)/shard_map/ppermute | solution.py:42
  34.7 7.3 %collective-permute-start.7 = (f32[512,256]{1,0:T(8,128)S(1)}, f32[512,256]{1,0:T(8,128)S(1)}, u32[]{:S(2)}, u32[]{:S(2)}) collective-permute-start(f32[512,256]{1,0:T(8,128)S(1)} %constant_dynamic-update-slice_fusion.2), channel_id=1, source_target_pairs={{0,2},{1,3},{2,0},{3,1},{4,6},{5,7},{6,4},{7,5},{8,10},{9,11},{10,... | collective-permute-start | bytes 1572872 | tf_op jit(solution)/shard_map/ppermute | solution.py:42
  39.3 15.0 %collective-permute-start.11 = (f32[512,256]{1,0:T(8,128)S(1)}, f32[512,256]{1,0:T(8,128)S(1)}, u32[]{:S(2)}, u32[]{:S(2)}) collective-permute-start(f32[512,256]{1,0:T(8,128)S(1)} %constant_dynamic-update-slice_fusion.2), channel_id=1, source_target_pairs={{0,128},{1,129},{2,130},{3,131},{4,132},{5,133},{6,134},{7,135},{8... | collective-permute-start | bytes 1572872 | tf_op jit(solution)/shard_map/ppermute | solution.py:42
  42.0 6.7 %copy-start.1 = (f32[1,64,128,128]{3,2,1,0:T(8,128)S(1)}, f32[1,64,128,128]{3,2,1,0:T(8,128)}, u32[]{:S(2)}) copy-start(f32[1,64,128,128]{3,2,1,0:T(8,128)} %param.19) | copy-start | bytes 12582916
  42.1 27.0 %collective-permute-start.9 = (f32[2,512,256]{2,1,0:T(8,128)S(1)}, f32[2,512,256]{2,1,0:T(8,128)S(1)}, u32[]{:S(2)}, u32[]{:S(2)}) collective-permute-start(f32[2,512,256]{2,1,0:T(8,128)S(1)} %pad_maximum_fusion.1.rest_0_), channel_id=1, source_target_pairs={{0,64},{1,65},{2,194},{3,195},{4,68},{5,69},{6,198},{7,199},{8,72}... | collective-permute-start | bytes 3145736 | tf_op jit(solution)/shard_map/ppermute | solution.py:42
  43.5 24.8 %collective-permute-start.10 = (f32[768,256]{1,0:T(8,128)S(1)}, f32[768,256]{1,0:T(8,128)S(1)}, u32[]{:S(2)}, u32[]{:S(2)}) collective-permute-start(f32[768,256]{1,0:T(8,128)S(1)} %copy-done.4), channel_id=1, source_target_pairs={{0,1},{1,0},{2,3},{3,2},{4,5},{5,4},{6,7},{7,6},{8,9},{9,8},{10,11... | collective-permute-start | bytes 2359304 | tf_op jit(solution)/shard_map/ppermute | solution.py:42
  54.3 14.8 %collective-permute-start.12 = (f32[512,256]{1,0:T(8,128)S(1)}, f32[512,256]{1,0:T(8,128)S(1)}, u32[]{:S(2)}, u32[]{:S(2)}) collective-permute-start(f32[512,256]{1,0:T(8,128)S(1)} %get-tuple-element.41.rest_3_), channel_id=1, source_target_pairs={{0,2},{2,4},{4,6},{6,8},{8,10},{10,12},{12,14},{14,16},{16,18},{18... | collective-permute-start | bytes 1572872 | tf_op jit(solution)/shard_map/ppermute | solution.py:435
  56.8 12.3 %collective-permute-start.13 = (f32[512,256]{1,0:T(8,128)S(1)}, f32[512,256]{1,0:T(8,128)S(1)}, u32[]{:S(2)}, u32[]{:S(2)}) collective-permute-start(f32[512,256]{1,0:T(8,128)S(1)} %get-tuple-element.42.rest_0_), channel_id=1, source_target_pairs={{2,0},{4,2},{6,4},{8,6},{10,8},{12,10},{14,12},{16,14},{18,16},{20... | collective-permute-start | bytes 1572872 | tf_op jit(solution)/shard_map/ppermute | solution.py:436
  69.1 7.4 %collective-permute-start.15 = (f32[2,512,256]{2,1,0:T(8,128)S(1)}, f32[2,512,256]{2,1,0:T(8,128)S(1)}, u32[]{:S(2)}, u32[]{:S(2)}) collective-permute-start(f32[2,512,256]{2,1,0:T(8,128)S(1)} %collective-permute-done.9.rest_3_), channel_id=1, source_target_pairs={{0,2},{1,3},{2,0},{3,1},{4,6},{5,7},{6,4},{7,5},{8,10},{9,11},{10,... | collective-permute-start | bytes 3145736 | tf_op jit(solution)/shard_map/ppermute | solution.py:42
  71.5 5.0 %collective-permute-start.14 = (f32[512,256]{1,0:T(8,128)S(1)}, f32[512,256]{1,0:T(8,128)S(1)}, u32[]{:S(2)}, u32[]{:S(2)}) collective-permute-start(f32[512,256]{1,0:T(8,128)S(1)} %collective-permute-done.11.rest_1_), channel_id=1, source_target_pairs={{0,2},{1,3},{2,0},{3,1},{4,6},{5,7},{6,4},{7,5},{8,10},{9,11},{10,... | collective-permute-start | bytes 1572872 | tf_op jit(solution)/shard_map/ppermute | solution.py:42
  76.6 10.7 %copy-start.11 = (f32[256]{0:T(256)S(1)}, f32[256]{0:T(256)}, u32[]{:S(2)}) copy-start(f32[256]{0:T(256)} %param.27) | copy-start | bytes 3076
  83.1 4.2 %collective-permute-start.16 = (f32[32,128]{1,0:T(8,128)S(1)}, f32[32,128]{1,0:T(8,128)S(1)}, u32[]{:S(2)}, u32[]{:S(2)}) collective-permute-start(f32[32,128]{1,0:T(8,128)S(1)} %get-tuple-element.50.refs_1_), channel_id=1, source_target_pairs={{0,1},{1,0},{2,3},{3,2},{4,5},{5,4},{6,7},{7,6},{8,9},{9,8},{10,11... | collective-permute-start | bytes 49160 | tf_op jit(solution)/shard_map/ppermute | solution.py:42
  (10 other events, 38.8 us)

commit v4 on v3

--- a/solution.py
+++ b/solution.py
@@ -107,13 +107,14 @@
     return dot(left, right)
 
 
-def chosen(y, mask_row, token_y):
-    here = jnp.broadcast_to(mask_row, (128, 128)).T
-    halves = []
-    for k in range(y.shape[1] // 128):
-        lanes = slice(k * 128, (k + 1) * 128)
-        halves.append(jnp.where(here == 1.0, token_y[:, lanes], y[:, lanes]))
-    return jnp.concatenate(halves, 1)
+def columns(mask):
+    n = mask.shape[0]
+    pad = jnp.zeros((128 - n, 128), F32)
+    return jnp.concatenate([mask[...].astype(F32), pad], 0).T
+
+
+def chosen(y, column, token_y):
+    return jnp.where(column == 1.0, token_y, y)
 
 
 def mix_into(xf, xg, weight, mask, token_y, store):
@@ -123,7 +124,7 @@
         y = mix_rows(xf[at, :], xg[at, :], weight)
         for j in range(step // 128):
             b = i * (step // 128) + j
-            store(b, chosen(y[j * 128 : (j + 1) * 128], mask[b : b + 1, :], token_y[:1, :]))
+            store(b, chosen(y[j * 128 : (j + 1) * 128], mask[:, b : b + 1], token_y[:1, :]))
 
 
 def mix_kernel(xf, xg, weight, mask, token_y, *outs):
@@ -134,7 +135,7 @@
                 out[pl.ds(b * 128, 128), :] = y
             b -= n
 
-    mix_into(xf, xg, weight, mask[...].astype(F32), token_y, store)
+    mix_into(xf, xg, weight, columns(mask), token_y, store)
 
 
 def mix(xf, xg, weight, mask, token_y, sizes):
@@ -190,7 +191,7 @@
         products, rows = [], []
         for u in range(UNROLL):
             k = i * UNROLL + u
-            t = index(k)
+            t = index(jnp.minimum(k, count - 1))
             product = tile_product(tile_of(t), y_of(t))
             products.append(jnp.where(k < count, product, 0.0))
             rows.append(row_of(t))
@@ -202,16 +203,11 @@
 
 
 def list_tiles(wanted, listed):
-    def clear(t, carry):
-        listed[t] = 0
-        return carry
-
     def step(t, n):
         listed[n] = t
         return n + jnp.where(wanted(t), 1, 0)
 
-    lax.fori_loop(0, listed.shape[0], clear, 0)
-    return lax.fori_loop(0, listed.shape[0] - UNROLL, step, 0)
+    return lax.fori_loop(0, listed.shape[0] - UNROLL, step, 0, unroll=8)
 
 
 def inside(col, low, high):
@@ -331,7 +327,7 @@
         copies.append(pltpu.make_async_copy(part, to, sems.at[k]))
         copies[-1].start()
     total[...] = total_in[...]
-    marks = mask[...].astype(F32)
+    marks = columns(mask)
     blocks = total.shape[0]
     for copy in copies:
         copy.wait()
@@ -369,7 +365,7 @@
     for b in range(blocks):
         at = pl.ds(b * 128, 128)
         v = total[b] + bias[...]
-        filled = chosen(features[at, :], marks[b : b + 1, :], token[...])
+        filled = chosen(features[at, :], marks[:, b : b + 1], token[...])
         h = filled + v / (1.0 + jnp.exp(-v))
         hidden[at, :] = h
         q = h * h

time: 90.3 us -> 88.5 us (0.980)
  the two profiles are of different devices: /device:TPU:1 before, /device:TPU:8 now
where the time goes in v4:
time: 88.5 us; the launch traced here: 86.9 us
  starting transfers between devices  33.8 us (38%)
  waiting for transfers between devices  27.3 us (31%)
  Pallas kernels  22.6 us (26%)
  local copies, waits for them, and re-layouts  2.03 us (2%)
  between operations  0.96 us (1%)
    ppermute x15, starting transfers between devices, send(): return lax.ppermute(value, BOTH, shift(move))  26.1 us
    ppermute x15, waiting for transfers between devices, send(): return lax.ppermute(value, BOTH, shift(move))  23.8 us
    ppermute x1, starting transfers between devices, neighbours(): after = lax.ppermute(first, 'dom', [(i + 1, i) for i in range(doms - 1)])  5.75 us
    pallas_call x1, Pallas kernels, final(): pl.pallas_call(final_kernel, out_shape=[jax.ShapeDtypeStruct((n, half), F...  5.51 us
    pallas_call x1, Pallas kernels, late_sum(): pl.pallas_call(functools.partial(late_kernel, late), out_shape=jax.ShapeD...  4.23 us
    pallas_call x2, Pallas kernels, mix(): pl.pallas_call(mix_kernel, out_shape=[jax.ShapeDtypeStruct((size, half),...  3.48 us
    pallas_call x1, Pallas kernels, hub_rows_of(): pl.pallas_call(hub_rows_kernel, out_shape=jax.ShapeDtypeStruct((count + 8...  2.81 us
    pallas_call x1, Pallas kernels, early_sum(): pl.pallas_call(functools.partial(early_kernel, late), out_shape=jax.Shape...  2.62 us
  transfers between devices with their start and end apart: 17, of which 13 were waited for; matrix products, arithmetic and copies ran while one was open for 2% of the time, Pallas kernels for 14%

profile of v4, /device:TPU:8, one launch (start us, length us, event | category | flops | bytes accessed | tf_op | source)
XLA Modules:
  0.0 86.9 jit_solution(5670466527303610928)
XLA Ops:
  0.0 2.8 %hub_rows.2.own_f = f32[40,256]{1,0:T(8,128)} custom-call(s32[32]{0:T(128)} %ids.1, s32[2048]{0:T(1024)} %mask.1, f32[2048,256]{1,0:T(8,128)} %features.3, f32[1,256]{1,0:T(1,128)} %bitcast.18), custom_call_target="tpu_custom_call" | custom-call | flops 1 | bytes 1 | tf_op jit(solution)/shard_map/hub_rows/pallas_call | solution.py:85
  2.8 2.4 %collective-permute-start = (f32[40,256]{1,0:T(8,128)}, f32[40,256]{1,0:T(8,128)S(1)}, u32[]{:S(2)}, u32[]{:S(2)}) collective-permute-start(f32[40,256]{1,0:T(8,128)} %hub_rows.2.own_f), channel_id=1, source_target_pairs={{0,1},{1,0},{2,3},{3,2},{4,5},{5,4},{6,7},{7,6},{8,9},{9,8},{10,11... | collective-permute-start | bytes 122888 | tf_op jit(solution)/shard_map/ppermute | solution.py:42
  10.8 2.7 %collective-permute-start.8 = (f32[1280,256]{1,0:T(8,128)S(1)}, f32[1280,256]{1,0:T(8,128)}, u32[]{:S(2)}, u32[]{:S(2)}) collective-permute-start(f32[1280,256]{1,0:T(8,128)S(1)} %pad_maximum_fusion.xf), channel_id=1, source_target_pairs={{0,1},{1,0},{2,3},{3,2},{4,5},{5,4},{6,7},{7,6},{8,9},{9,8},{10,11... | collective-permute-start | bytes 3932168 | tf_op jit(solution)/shard_map/ppermute | solution.py:42
  13.5 2.1 %mix_hub.1 = (f32[64,256]{1,0:T(8,128)}, f32[8,256]{1,0:T(8,128)}) custom-call(f32[40,256]{1,0:T(8,128)} %hub_rows.2.own_f, f32[40,256]{1,0:T(8,128)} %copy-done.14, f32[40,256]{1,0:T(8,128)} %copy-done.15, f32[40,256]{1,0:T(8,128)} %copy-done.16, f32[512,256]{1,0:T(8,128)} %weight.5), custom_call_target="tpu_custom_call" | custom-call | flops 1 | bytes 1 | tf_op jit(solution)/shard_map/mix_hub/pallas_call | solution.py:167
  15.5 5.7 %collective-permute-start.3 = (f32[64,256]{1,0:T(8,128)}, f32[64,256]{1,0:T(8,128)S(1)}, u32[]{:S(2)}, u32[]{:S(2)}) collective-permute-start(f32[64,256]{1,0:T(8,128)} %get-tuple-element.31), channel_id=1, source_target_pairs={{0,16},{1,17},{2,18},{3,19},{4,20},{5,21},{6,22},{7,23},{8,24},{9,... | collective-permute-start | bytes 196616 | tf_op jit(solution)/shard_map/ppermute | solution.py:42
  22.1 1.9 %collective-permute-done.3 = f32[64,256]{1,0:T(8,128)S(1)} collective-permute-done((f32[64,256]{1,0:T(8,128)}, f32[64,256]{1,0:T(8,128)S(1)}, u32[]{:S(2)}, u32[]{:S(2)}) %collective-permute-start.3) | collective-permute-done | bytes 65568 | tf_op jit(solution)/shard_map/ppermute | solution.py:42
  25.0 3.6 %collective-permute-start.5 = (f32[128,256]{1,0:T(8,128)S(1)}, f32[128,256]{1,0:T(8,128)S(1)}, u32[]{:S(2)}, u32[]{:S(2)}) collective-permute-start(f32[128,256]{1,0:T(8,128)S(1)} %get-tuple-element.53), channel_id=1, source_target_pairs={{0,28},{1,29},{2,30},{3,31},{4,0},{5,1},{6,2},{7,3},{8,4},{9,5},{1... | collective-permute-start | bytes 393224 | tf_op jit(solution)/shard_map/ppermute | solution.py:42
  28.6 4.2 %collective-permute-done.4 = f32[128,256]{1,0:T(8,128)S(1)} collective-permute-done((f32[128,256]{1,0:T(8,128)S(1)}, f32[128,256]{1,0:T(8,128)S(1)}, u32[]{:S(2)}, u32[]{:S(2)}) %collective-permute-start.4) | collective-permute-done | bytes 131104 | tf_op jit(solution)/shard_map/ppermute | solution.py:42
  32.8 3.7 %collective-permute-done.6 = f32[128,256]{1,0:T(8,128)S(1)} collective-permute-done((f32[128,256]{1,0:T(8,128)S(1)}, f32[128,256]{1,0:T(8,128)S(1)}, u32[]{:S(2)}, u32[]{:S(2)}) %collective-permute-start.6) | collective-permute-done | bytes 131104 | tf_op jit(solution)/shard_map/ppermute | solution.py:42
  36.6 3.3 %collective-permute-start.11 = (f32[512,256]{1,0:T(8,128)S(1)}, f32[512,256]{1,0:T(8,128)S(1)}, u32[]{:S(2)}, u32[]{:S(2)}) collective-permute-start(f32[512,256]{1,0:T(8,128)S(1)} %constant_dynamic-update-slice_fusion.2), channel_id=1, source_target_pairs={{0,128},{1,129},{2,130},{3,131},{4,132},{5,133},{6,134},{7,135},{8... | collective-permute-start | bytes 1572872 | tf_op jit(solution)/shard_map/ppermute | solution.py:42
  44.3 2.6 %mix_rows.3 = (f32[512,256]{1,0:T(8,128)S(1)}, f32[128,256]{1,0:T(8,128)S(1)}, f32[128,256]{1,0:T(8,128)S(1)}, f32[512,256]{1,0:T(8,128)S(1)}) custom-call(f32[1280,256]{1,0:T(8,128)S(1)} %pad_maximum_fusion.xf, f32[1280,256]{1,0:T(8,128)} %collective-permute-done.8.xg, f32[512,256]{1,0:T(8,128)S(1)} %copy-done.2, s32[10,128]{1,0:T(8,128)S(1)} %pad_add_fusion.mask, ...), custom_call_target="tpu_custom_call" | custom-call | flops 1 | bytes 1 | tf_op jit(solution)/shard_map/mix_rows/pallas_call | solution.py:143
  46.9 2.6 %early_tiles.1.total_in = f32[16,128,256]{2,1,0:T(8,128)S(1)} custom-call(s32[1,64]{1,0:T(1,128)S(1)} %copy-done.8, s32[1,64]{1,0:T(1,128)S(1)} %copy-done.9, f32[64,128,128]{2,1,0:T(8,128)S(1)} %bitcast.14, f32[512,256]{1,0:T(8,128)S(1)} %get-tuple-element.42.rest_0_, f32[128,256]{1,0:T(8,128)S(1)} %get-tuple-element.39.rest_1_, ...), custom_call_target="tpu_custom_call" | custom-call | flops 1 | bytes 1 | tf_op jit(solution)/shard_map/early_tiles/pallas_call | solution.py:250
  49.5 3.0 %collective-permute-done.11.rest_1_ = f32[512,256]{1,0:T(8,128)S(1)} collective-permute-done((f32[512,256]{1,0:T(8,128)S(1)}, f32[512,256]{1,0:T(8,128)S(1)}, u32[]{:S(2)}, u32[]{:S(2)}) %collective-permute-start.11) | collective-permute-done | bytes 524320 | tf_op jit(solution)/shard_map/ppermute | solution.py:42
  52.6 1.9 %collective-permute-start.12 = (f32[512,256]{1,0:T(8,128)S(1)}, f32[512,256]{1,0:T(8,128)S(1)}, u32[]{:S(2)}, u32[]{:S(2)}) collective-permute-start(f32[512,256]{1,0:T(8,128)S(1)} %get-tuple-element.41.rest_3_), channel_id=1, source_target_pairs={{0,2},{2,4},{4,6},{6,8},{8,10},{10,12},{12,14},{14,16},{16,18},{18... | collective-permute-start | bytes 1572872 | tf_op jit(solution)/shard_map/ppermute | solution.py:431
  54.5 5.8 %collective-permute-start.13 = (f32[512,256]{1,0:T(8,128)S(1)}, f32[512,256]{1,0:T(8,128)S(1)}, u32[]{:S(2)}, u32[]{:S(2)}) collective-permute-start(f32[512,256]{1,0:T(8,128)S(1)} %get-tuple-element.42.rest_0_), channel_id=1, source_target_pairs={{2,0},{4,2},{6,4},{8,6},{10,8},{12,10},{14,12},{16,14},{18,16},{20... | collective-permute-start | bytes 1572872 | tf_op jit(solution)/shard_map/ppermute | solution.py:432
  60.3 2.3 %collective-permute-done.10.xg = f32[768,256]{1,0:T(8,128)S(1)} collective-permute-done((f32[768,256]{1,0:T(8,128)S(1)}, f32[768,256]{1,0:T(8,128)S(1)}, u32[]{:S(2)}, u32[]{:S(2)}) %collective-permute-start.10) | collective-permute-done | bytes 786464 | tf_op jit(solution)/shard_map/ppermute | solution.py:42
  63.5 1.8 %collective-permute-done.12.prev = f32[512,256]{1,0:T(8,128)S(1)} collective-permute-done((f32[512,256]{1,0:T(8,128)S(1)}, f32[512,256]{1,0:T(8,128)S(1)}, u32[]{:S(2)}, u32[]{:S(2)}) %collective-permute-start.12) | collective-permute-done | bytes 524320 | tf_op jit(solution)/shard_map/ppermute | solution.py:431
  65.3 1.7 %collective-permute-done.13.after = f32[512,256]{1,0:T(8,128)S(1)} collective-permute-done((f32[512,256]{1,0:T(8,128)S(1)}, f32[512,256]{1,0:T(8,128)S(1)}, u32[]{:S(2)}, u32[]{:S(2)}) %collective-permute-start.13) | collective-permute-done | bytes 524320 | tf_op jit(solution)/shard_map/ppermute | solution.py:432
  67.0 1.6 %collective-permute-done.9.rest_3_ = f32[2,512,256]{2,1,0:T(8,128)S(1)} collective-permute-done((f32[2,512,256]{2,1,0:T(8,128)S(1)}, f32[2,512,256]{2,1,0:T(8,128)S(1)}, u32[]{:S(2)}, u32[]{:S(2)}) %collective-permute-start.9) | collective-permute-done | bytes 1048608 | tf_op jit(solution)/shard_map/ppermute | solution.py:42
  69.8 4.2 %late_tiles.1.total_in = f32[16,128,256]{2,1,0:T(8,128)S(1)} custom-call(s32[1,64]{1,0:T(1,128)S(1)} %copy-done.8, s32[1,64]{1,0:T(1,128)S(1)} %copy-done.9, f32[64,128,128]{2,1,0:T(8,128)S(1)} %bitcast.15, f32[512,256]{1,0:T(8,128)S(1)} %collective-permute-done.12.prev, f32[512,256]{1,0:T(8,128)S(1)} %collective-permute-done.13.after, ...), custom_call_target="tpu_custom_call" | custom-call | flops 1 | bytes 1 | tf_op jit(solution)/shard_map/late_tiles/pallas_call | solution.py:300
  74.1 5.5 %final_tiles.1 = (f32[2048,256]{1,0:T(8,128)S(1)}, f32[32,128]{1,0:T(8,128)S(1)}) custom-call(s32[1]{0:T(128)S(6)} %copy.20.live_ref, s32[1,64]{1,0:T(1,128)S(1)} %copy-done.12, s32[1,64]{1,0:T(1,128)S(1)} %copy-done.13, f32[64,128,128]{2,1,0:T(8,128)S(1)} %bitcast.16, s32[16,128]{1,0:T(8,128)S(1)} %bitcast.17, f32[1,256]{1,0:T(1,128)S(1)} %bitcast.19, ...), custom_call_target="tpu_custom_call" | custom-call | flops 1 | bytes 1 | tf_op jit(solution)/shard_map/final_tiles/pallas_call | solution.py:382
  79.6 2.5 %collective-permute-start.16 = (f32[32,128]{1,0:T(8,128)S(1)}, f32[32,128]{1,0:T(8,128)S(1)}, u32[]{:S(2)}, u32[]{:S(2)}) collective-permute-start(f32[32,128]{1,0:T(8,128)S(1)} %get-tuple-element.50.refs_1_), channel_id=1, source_target_pairs={{0,1},{1,0},{2,3},{3,2},{4,5},{5,4},{6,7},{7,6},{8,9},{9,8},{10,11... | collective-permute-start | bytes 49160 | tf_op jit(solution)/shard_map/ppermute | solution.py:42
  82.2 2.8 %collective-permute-done.16.refs_2_ = f32[32,128]{1,0:T(8,128)S(1)} collective-permute-done((f32[32,128]{1,0:T(8,128)S(1)}, f32[32,128]{1,0:T(8,128)S(1)}, u32[]{:S(2)}, u32[]{:S(2)}) %collective-permute-start.16) | collective-permute-done | bytes 16416 | tf_op jit(solution)/shard_map/ppermute | solution.py:42
  85.0 1.9 %normalise.1 = f32[2048,256]{1,0:T(8,128)} custom-call(f32[2048,256]{1,0:T(8,128)S(1)} %get-tuple-element.49.refs_0_, f32[32,128]{1,0:T(8,128)S(1)} %get-tuple-element.50.refs_1_, f32[32,128]{1,0:T(8,128)S(1)} %collective-permute-done.16.refs_2_, f32[1,256]{1,0:T(1,128)S(1)} %bitcast.21), custom_call_target="tpu_custom_call" | custom-call | flops 1 | bytes 1 | tf_op jit(solution)/shard_map/normalise/pallas_call | solution.py:418
  (64 shorter events, 13.3 us)
Async XLA Ops:
  0.0 7.0 %copy-start = (f32[2048,256]{1,0:T(8,128)S(1)}, f32[2048,256]{1,0:T(8,128)}, u32[]{:S(2)}) copy-start(f32[2048,256]{1,0:T(8,128)} %features.3) | copy-start | bytes 6291460
  2.8 5.8 %collective-permute-start = (f32[40,256]{1,0:T(8,128)}, f32[40,256]{1,0:T(8,128)S(1)}, u32[]{:S(2)}, u32[]{:S(2)}) collective-permute-start(f32[40,256]{1,0:T(8,128)} %hub_rows.2.own_f), channel_id=1, source_target_pairs={{0,1},{1,0},{2,3},{3,2},{4,5},{5,4},{6,7},{7,6},{8,9},{9,8},{10,11... | collective-permute-start | bytes 122888 | tf_op jit(solution)/shard_map/ppermute | solution.py:42
  5.2 4.2 %collective-permute-start.1 = (f32[40,256]{1,0:T(8,128)}, f32[40,256]{1,0:T(8,128)S(1)}, u32[]{:S(2)}, u32[]{:S(2)}) collective-permute-start(f32[40,256]{1,0:T(8,128)} %hub_rows.2.own_f), channel_id=1, source_target_pairs={{0,32},{1,33},{2,34},{3,35},{4,36},{5,37},{6,38},{7,39},{8,40},{9,... | collective-permute-start | bytes 122888 | tf_op jit(solution)/shard_map/ppermute | solution.py:42
  6.6 4.2 %collective-permute-start.2 = (f32[40,256]{1,0:T(8,128)}, f32[40,256]{1,0:T(8,128)S(1)}, u32[]{:S(2)}, u32[]{:S(2)}) collective-permute-start(f32[40,256]{1,0:T(8,128)} %hub_rows.2.own_f), channel_id=1, source_target_pairs={{0,33},{1,32},{2,35},{3,34},{4,37},{5,36},{6,39},{7,38},{8,41},{9,... | collective-permute-start | bytes 122888 | tf_op jit(solution)/shard_map/ppermute | solution.py:42
  8.1 36.1 %copy-start.5 = (s32[2048]{0:T(1024)S(1)}, s32[2048]{0:T(1024)}, u32[]{:S(2)}) copy-start(s32[2048]{0:T(1024)} %mask.1) | copy-start | bytes 24580
  10.8 30.7 %collective-permute-start.8 = (f32[1280,256]{1,0:T(8,128)S(1)}, f32[1280,256]{1,0:T(8,128)}, u32[]{:S(2)}, u32[]{:S(2)}) collective-permute-start(f32[1280,256]{1,0:T(8,128)S(1)} %pad_maximum_fusion.xf), channel_id=1, source_target_pairs={{0,1},{1,0},{2,3},{3,2},{4,5},{5,4},{6,7},{7,6},{8,9},{9,8},{10,11... | collective-permute-start | bytes 3932168 | tf_op jit(solution)/shard_map/ppermute | solution.py:42
  15.5 27.6 %copy-start.4 = (f32[768,256]{1,0:T(8,128)S(1)}, f32[768,256]{1,0:T(8,128)}, u32[]{:S(2)}) copy-start(f32[768,256]{1,0:T(8,128)} %slice.53.xf) | copy-start | bytes 2359300
  15.5 28.7 %copy-start.2 = (f32[512,256]{1,0:T(8,128)S(1)}, f32[512,256]{1,0:T(8,128)}, u32[]{:S(2)}) copy-start(f32[512,256]{1,0:T(8,128)} %weight.5) | copy-start | bytes 1572868
  15.5 28.7 %copy-start.6 = (f32[8,256]{1,0:T(8,128)S(1)}, f32[8,256]{1,0:T(8,128)}, u32[]{:S(2)}) copy-start(f32[8,256]{1,0:T(8,128)} %get-tuple-element.35.token_y) | copy-start | bytes 24580
  15.5 8.5 %collective-permute-start.3 = (f32[64,256]{1,0:T(8,128)}, f32[64,256]{1,0:T(8,128)S(1)}, u32[]{:S(2)}, u32[]{:S(2)}) collective-permute-start(f32[64,256]{1,0:T(8,128)} %get-tuple-element.31), channel_id=1, source_target_pairs={{0,16},{1,17},{2,18},{3,19},{4,20},{5,21},{6,22},{7,23},{8,24},{9,... | collective-permute-start | bytes 196616 | tf_op jit(solution)/shard_map/ppermute | solution.py:42
  24.0 8.8 %collective-permute-start.4 = (f32[128,256]{1,0:T(8,128)S(1)}, f32[128,256]{1,0:T(8,128)S(1)}, u32[]{:S(2)}, u32[]{:S(2)}) collective-permute-start(f32[128,256]{1,0:T(8,128)S(1)} %get-tuple-element.53), channel_id=1, source_target_pairs={{0,4},{1,5},{2,6},{3,7},{4,8},{5,9},{6,10},{7,11},{8,12},{9,13},{1... | collective-permute-start | bytes 393224 | tf_op jit(solution)/shard_map/ppermute | solution.py:42
  25.0 7.8 %collective-permute-start.5 = (f32[128,256]{1,0:T(8,128)S(1)}, f32[128,256]{1,0:T(8,128)S(1)}, u32[]{:S(2)}, u32[]{:S(2)}) collective-permute-start(f32[128,256]{1,0:T(8,128)S(1)} %get-tuple-element.53), channel_id=1, source_target_pairs={{0,28},{1,29},{2,30},{3,31},{4,0},{5,1},{6,2},{7,3},{8,4},{9,5},{1... | collective-permute-start | bytes 393224 | tf_op jit(solution)/shard_map/ppermute | solution.py:42
  28.6 8.0 %collective-permute-start.6 = (f32[128,256]{1,0:T(8,128)S(1)}, f32[128,256]{1,0:T(8,128)S(1)}, u32[]{:S(2)}, u32[]{:S(2)}) collective-permute-start(f32[128,256]{1,0:T(8,128)S(1)} %get-tuple-element.53), channel_id=1, source_target_pairs={{0,8},{1,9},{2,10},{3,11},{4,12},{5,13},{6,14},{7,15},{8,16},{9,17... | collective-permute-start | bytes 393224 | tf_op jit(solution)/shard_map/ppermute | solution.py:42
  36.5 3.4 %collective-permute-start.7 = (f32[512,256]{1,0:T(8,128)S(1)}, f32[512,256]{1,0:T(8,128)S(1)}, u32[]{:S(2)}, u32[]{:S(2)}) collective-permute-start(f32[512,256]{1,0:T(8,128)S(1)} %constant_dynamic-update-slice_fusion.2), channel_id=1, source_target_pairs={{0,2},{1,3},{2,0},{3,1},{4,6},{5,7},{6,4},{7,5},{8,10},{9,11},{10,... | collective-permute-start | bytes 1572872 | tf_op jit(solution)/shard_map/ppermute | solution.py:42
  36.6 16.0 %collective-permute-start.11 = (f32[512,256]{1,0:T(8,128)S(1)}, f32[512,256]{1,0:T(8,128)S(1)}, u32[]{:S(2)}, u32[]{:S(2)}) collective-permute-start(f32[512,256]{1,0:T(8,128)S(1)} %constant_dynamic-update-slice_fusion.2), channel_id=1, source_target_pairs={{0,128},{1,129},{2,130},{3,131},{4,132},{5,133},{6,134},{7,135},{8... | collective-permute-start | bytes 1572872 | tf_op jit(solution)/shard_map/ppermute | solution.py:42
  41.5 5.4 %copy-start.1 = (f32[1,64,128,128]{3,2,1,0:T(8,128)S(1)}, f32[1,64,128,128]{3,2,1,0:T(8,128)}, u32[]{:S(2)}) copy-start(f32[1,64,128,128]{3,2,1,0:T(8,128)} %param.19) | copy-start | bytes 12582916
  41.6 27.0 %collective-permute-start.9 = (f32[2,512,256]{2,1,0:T(8,128)S(1)}, f32[2,512,256]{2,1,0:T(8,128)S(1)}, u32[]{:S(2)}, u32[]{:S(2)}) collective-permute-start(f32[2,512,256]{2,1,0:T(8,128)S(1)} %pad_maximum_fusion.1.rest_0_), channel_id=1, source_target_pairs={{0,64},{1,65},{2,194},{3,195},{4,68},{5,69},{6,198},{7,199},{8,72}... | collective-permute-start | bytes 3145736 | tf_op jit(solution)/shard_map/ppermute | solution.py:42
  43.1 19.4 %collective-permute-start.10 = (f32[768,256]{1,0:T(8,128)S(1)}, f32[768,256]{1,0:T(8,128)S(1)}, u32[]{:S(2)}, u32[]{:S(2)}) collective-permute-start(f32[768,256]{1,0:T(8,128)S(1)} %copy-done.4), channel_id=1, source_target_pairs={{0,1},{1,0},{2,3},{3,2},{4,5},{5,4},{6,7},{7,6},{8,9},{9,8},{10,11... | collective-permute-start | bytes 2359304 | tf_op jit(solution)/shard_map/ppermute | solution.py:42
  52.6 12.7 %collective-permute-start.12 = (f32[512,256]{1,0:T(8,128)S(1)}, f32[512,256]{1,0:T(8,128)S(1)}, u32[]{:S(2)}, u32[]{:S(2)}) collective-permute-start(f32[512,256]{1,0:T(8,128)S(1)} %get-tuple-element.41.rest_3_), channel_id=1, source_target_pairs={{0,2},{2,4},{4,6},{6,8},{8,10},{10,12},{12,14},{14,16},{16,18},{18... | collective-permute-start | bytes 1572872 | tf_op jit(solution)/shard_map/ppermute | solution.py:431
  54.5 12.5 %collective-permute-start.13 = (f32[512,256]{1,0:T(8,128)S(1)}, f32[512,256]{1,0:T(8,128)S(1)}, u32[]{:S(2)}, u32[]{:S(2)}) collective-permute-start(f32[512,256]{1,0:T(8,128)S(1)} %get-tuple-element.42.rest_0_), channel_id=1, source_target_pairs={{2,0},{4,2},{6,4},{8,6},{10,8},{12,10},{14,12},{16,14},{18,16},{20... | collective-permute-start | bytes 1572872 | tf_op jit(solution)/shard_map/ppermute | solution.py:432
  68.6 5.5 %collective-permute-start.15 = (f32[2,512,256]{2,1,0:T(8,128)S(1)}, f32[2,512,256]{2,1,0:T(8,128)S(1)}, u32[]{:S(2)}, u32[]{:S(2)}) collective-permute-start(f32[2,512,256]{2,1,0:T(8,128)S(1)} %collective-permute-done.9.rest_3_), channel_id=1, source_target_pairs={{0,2},{1,3},{2,0},{3,1},{4,6},{5,7},{6,4},{7,5},{8,10},{9,11},{10,... | collective-permute-start | bytes 3145736 | tf_op jit(solution)/shard_map/ppermute | solution.py:42
  68.6 5.5 %collective-permute-start.14 = (f32[512,256]{1,0:T(8,128)S(1)}, f32[512,256]{1,0:T(8,128)S(1)}, u32[]{:S(2)}, u32[]{:S(2)}) collective-permute-start(f32[512,256]{1,0:T(8,128)S(1)} %collective-permute-done.11.rest_1_), channel_id=1, source_target_pairs={{0,2},{1,3},{2,0},{3,1},{4,6},{5,7},{6,4},{7,5},{8,10},{9,11},{10,... | collective-permute-start | bytes 1572872 | tf_op jit(solution)/shard_map/ppermute | solution.py:42
  74.1 10.9 %copy-start.11 = (f32[256]{0:T(256)S(1)}, f32[256]{0:T(256)}, u32[]{:S(2)}) copy-start(f32[256]{0:T(256)} %param.27) | copy-start | bytes 3076
  79.6 5.3 %collective-permute-start.16 = (f32[32,128]{1,0:T(8,128)S(1)}, f32[32,128]{1,0:T(8,128)S(1)}, u32[]{:S(2)}, u32[]{:S(2)}) collective-permute-start(f32[32,128]{1,0:T(8,128)S(1)} %get-tuple-element.50.refs_1_), channel_id=1, source_target_pairs={{0,1},{1,0},{2,3},{3,2},{4,5},{5,4},{6,7},{7,6},{8,9},{9,8},{10,11... | collective-permute-start | bytes 49160 | tf_op jit(solution)/shard_map/ppermute | solution.py:42
  (10 other events, 43.8 us)
